TPU v7x, 32 devices: a whole 2x2x4 slice. The times are simulated.
32 devices in a mesh: dp: 8 (over z, y), mp: 4 (over x, core).
Axes of the slice: x: 2, y: 2, z: 4, core: 2. Of those that a mesh axis runs over, the one named last changes fastest.
Arguments:
- output_gradient: bfloat16 [1536, 3584], P('dp', 'mp'), may hold values from -6 to 6
- gate_preactivation: bfloat16 [1536, 9984], P('dp', 'mp'), may hold values from -8 to 8
- up_preactivation: bfloat16 [1536, 9984], P('dp', 'mp'), may hold values from -6 to 6
- down_weight: bfloat16 [9984, 3584], P('mp'), may hold values from -0.0625 to 0.0625
- adapter_first: bfloat16 [9984, 96], P('mp'), may hold values from -0.0625 to 0.0625
- adapter_second: bfloat16 [96, 3584], replicated, may hold values from -0.09375 to 0.09375
- plan: int32 [192], P('dp'), may hold values from 0 to 7, as said below
Outputs:
- grad_gate: bfloat16 [1536, 9984], P('dp', 'mp')
- grad_up: bfloat16 [1536, 9984], P('dp', 'mp')
- grad_a: float32 [4, 2496, 96], P('mp', 'dp')
- grad_b: float32 [96, 3584], P('dp')
Inputs may be any that keep to these rules, and one draw needn't show every extreme that they name: Every owner 0 to 7 is named by exactly 24 blocks; of the 24 blocks of one device (plan rows of one index of dp) at most 3 name the same owner, and in every draw some device's blocks name one owner exactly 3 times.
All inputs are finite; a program needn't handle non-finite values.
Results may differ from a plain program's by a relative error of at most 0.005.
Values may be sent and summed in bfloat16 or wider, within the bound.
No kernel may reach another device: no remote copies, remote signals or barrier semaphores. Data moves between devices by JAX's collectives and lax.ppermute only.
A program may use at most 64 MiB of HBM per device.

v0:
```python
import jax
import jax.numpy as jnp
from jax import lax
from jax.sharding import PartitionSpec as P


def body(
    output_gradient,
    gate_preactivation,
    up_preactivation,
    down_weight,
    adapter_first,
    adapter_second,
    plan,
):
    groups = lax.axis_size("dp")
    owned = plan.shape[0]
    capacity = -(-owned // groups)
    tokens_here = output_gradient.shape[0]
    feature_cols = output_gradient.shape[1]
    block_width = tokens_here // owned * feature_cols
    slot_count = groups * capacity
    positions = jnp.arange(owned, dtype=jnp.int32)
    earlier = (plan[None, :] == plan[:, None]) & (positions[None, :] < positions[:, None])
    target = plan * capacity + jnp.sum(earlier.astype(jnp.int32), axis=1)
    sending = target[None, :] == jnp.arange(slot_count, dtype=jnp.int32)[:, None]
    outgoing = jnp.dot(
        sending.astype(jnp.bfloat16),
        output_gradient.reshape(owned, block_width),
        preferred_element_type=jnp.float32,
    ).astype(jnp.bfloat16)
    filled = jnp.sum(sending.astype(jnp.float32), axis=1).astype(jnp.bfloat16)
    arrived, present = (
        lax.all_to_all(outgoing, "dp", split_axis=0, concat_axis=0, tiled=True),
        lax.all_to_all(filled, "dp", split_axis=0, concat_axis=0, tiled=True),
    )
    present_flag = present.astype(jnp.int32)
    ranking = jnp.cumsum(present_flag) - 1
    keeping = (ranking[None, :] == positions[:, None]) & (present_flag[None, :] > 0)
    packed_tokens = (
        jnp.dot(keeping.astype(jnp.bfloat16), arrived, preferred_element_type=jnp.float32)
        .astype(jnp.bfloat16)
        .reshape(tokens_here, feature_cols)
    )
    feature_rows = lax.all_gather(packed_tokens, "mp", axis=1, tiled=True)
    gate_vals = gate_preactivation.astype(jnp.float32)
    up_vals = up_preactivation.astype(jnp.float32)
    sigmoid_gate = jax.nn.sigmoid(gate_vals)
    silu_gate = gate_vals * sigmoid_gate
    hidden_units = (silu_gate * up_vals).astype(jnp.bfloat16)
    low_rank_piece = jnp.dot(hidden_units, adapter_first, preferred_element_type=jnp.float32)
    low_rank_rows = lax.psum(low_rank_piece, "mp").astype(jnp.bfloat16)
    passed_through = lax.dot_general(
        feature_rows, adapter_second, (((1,), (1,)), ((), ())), preferred_element_type=jnp.float32
    ).astype(jnp.bfloat16)
    grad_a_rows = lax.psum_scatter(
        lax.dot_general(
            hidden_units,
            passed_through,
            (((0,), (0,)), ((), ())),
            preferred_element_type=jnp.float32,
        ),
        "dp",
        scatter_dimension=0,
        tiled=True,
    )
    part_rows = lax.psum_scatter(
        lax.dot_general(
            low_rank_rows,
            packed_tokens,
            (((0,), (0,)), ((), ())),
            preferred_element_type=jnp.float32,
        ),
        "dp",
        scatter_dimension=0,
        tiled=True,
    )
    grad_b_rows = lax.all_gather(part_rows, "mp", axis=1, tiled=True)
    hidden_gradient = lax.dot_general(
        feature_rows, down_weight, (((1,), (1,)), ((), ())), preferred_element_type=jnp.float32
    )
    hidden_gradient = hidden_gradient + lax.dot_general(
        passed_through, adapter_first, (((1,), (1,)), ((), ())), preferred_element_type=jnp.float32
    )
    grad_gate = (
        hidden_gradient * up_vals * sigmoid_gate * (1.0 + gate_vals * (1.0 - sigmoid_gate))
    ).astype(jnp.bfloat16)
    grad_up = (hidden_gradient * silu_gate).astype(jnp.bfloat16)
    return (grad_gate, grad_up, grad_a_rows[None], grad_b_rows)


def solution(mesh):
    return jax.shard_map(
        body,
        mesh=mesh,
        in_specs=(
            P("dp", "mp"),
            P("dp", "mp"),
            P("dp", "mp"),
            P("mp", None),
            P("mp", None),
            P(),
            P("dp"),
        ),
        out_specs=(P("dp", "mp"), P("dp", "mp"), P("mp", "dp", None), P("dp", None)),
        check_vma=False,
    )
```

profile of v0, /device:TPU:0, one launch (start us, length us, event | category | flops | bytes accessed | tf_op | source)
XLA Modules:
  0.0 165.8 jit_solution(9476661914861650010)
XLA Ops:
  7.2 0.0 copy-start
  7.2 0.9 convert_reduce_fusion.1
  8.1 0.7 multiply_add_fusion
  8.8 0.1 convert_reduce_fusion
  8.9 0.7 convert_element_type.87
  9.6 7.3 %all-to-all-start = ((bf16[8,3,1]{1,2,0:T(2,128)(2,1)}), bf16[8,3,1]{1,2,0:T(2,128)(2,1)S(1)}, u32[]{:S(2)}, u32[]{:S(2)}) async-start(bf16[8,3,1]{1,2,0:T(2,128)(2,1)} %convert_element_type.87), calls=%async_computation | async-start | bytes 8192 | tf_op jit(solution)/shard_map/all_to_all | solution.py:35
  16.9 1.1 reshape.77
  18.0 0.2 convolution_convert_fusion.1
  18.3 1.0 all_to_all.13
  19.2 4.1 %all-to-all-done = bf16[8,3,1]{1,2,0:T(2,128)(2,1)S(1)} async-done(((bf16[8,3,1]{1,2,0:T(2,128)(2,1)}), bf16[8,3,1]{1,2,0:T(2,128)(2,1)S(1)}, u32[]{:S(2)}, u32[]{:S(2)}) %all-to-all-start) | async-done | bytes 80 | tf_op jit(solution)/shard_map/all_to_all | solution.py:35
  23.3 3.5 %all-to-all-start.1 = ((bf16[8,3,7168]{2,1,0:T(4,128)(2,1)}), bf16[8,3,7168]{2,1,0:T(4,128)(2,1)S(1)}, u32[]{:S(2)}, u32[]{:S(2)}) async-start(bf16[8,3,7168]{2,1,0:T(4,128)(2,1)} %all_to_all.13), calls=%async_computation.1 | async-start | bytes 917504 | tf_op jit(solution)/shard_map/all_to_all | solution.py:34
  26.8 0.0 all-gather.2.cloned.1.call-start
  26.9 0.1 reshape.80
  27.0 0.1 gt.12
  27.1 0.1 add_reduce_fusion
  27.2 11.4 %all-to-all-done.1 = bf16[8,3,7168]{2,1,0:T(4,128)(2,1)S(1)} async-done(((bf16[8,3,7168]{2,1,0:T(4,128)(2,1)}), bf16[8,3,7168]{2,1,0:T(4,128)(2,1)S(1)}, u32[]{:S(2)}, u32[]{:S(2)}) %all-to-all-start.1) | async-done | bytes 344096 | tf_op jit(solution)/shard_map/all_to_all | solution.py:34
  38.6 0.3 all_to_all.15
  38.9 0.2 convolution_convert_fusion
  39.2 0.9 reshape.78
  40.1 0.0 all-gather.2.cloned.1.call-update
  40.1 0.0 all-reduce.5.cloned.1.call-start
  40.1 17.7 %all-gather.2.cloned.1.call-done = bf16[192,3584]{1,0:T(8,128)(2,1)} async-done(((bf16[192,896]{1,0:T(8,128)(2,1)}), bf16[192,3584]{1,0:T(8,128)(2,1)}) %all-gather.2.cloned.1.call-update) | async-done | bytes 1376272 | tf_op jit(solution)/shard_map/all_gather | solution.py:45
  57.9 0.0 copy-done
  57.9 0.0 copy-start.2
  57.9 1.9 %convolution_convert_fusion.2 = bf16[192,96]{1,0:T(8,128)(2,1)S(1)} fusion(bf16[192,3584]{1,0:T(8,128)(2,1)} %all-gather.2.cloned.1.call-done, bf16[96,3584]{1,0:T(8,128)(2,1)S(1)} %copy-done), kind=kOutput, calls=%fused_computation.17 | convolution fusion | flops 132139008 | bytes 2101248 | tf_op jit(solution)/shard_map/dot_general | solution.py:53
  59.8 0.0 copy-done.2
  59.8 0.0 copy-start.3
  59.8 10.8 %fusion.18 = f32[192,2496]{1,0:T(8,128)} fusion(bf16[192,3584]{1,0:T(8,128)(2,1)S(1)} %copy-done.2, bf16[2496,3584]{1,0:T(8,128)(2,1)} %param.10), kind=kOutput, calls=%fused_computation.37 | convolution fusion | flops 3435134976 | bytes 21184512 | tf_op jit(solution)/shard_map/dot_general | solution.py:79
  70.7 0.0 copy-done.3
  70.7 4.7 %multiply_convert_fusion = (bf16[192,2496]{1,0:T(8,128)(2,1)}, bf16[192,2496]{1,0:T(8,128)(2,1)}, bf16[192,2496]{1,0:T(8,128)(2,1)S(1)}) fusion(bf16[192,2496]{1,0:T(8,128)(2,1)} %param.8, bf16[192,2496]{1,0:T(8,128)(2,1)} %param.9, f32[192,2496]{1,0:T(8,128)} %fusion.18, bf16[192,96]{1,0:T(8,128)(2,1)S(1)} %convolution_convert_fusion.2, ...), kind=kOutput, calls=%fused_computation.16 | convolution fusion | flops 100638720 | bytes 7225344 | tf_op jit(solution)/shard_map/dot_general | solution.py:82
  75.4 1.3 fusion.19
  76.7 0.0 all-reduce.5.cloned.1.call-update
  76.7 0.4 fusion.20
  77.2 11.6 %psum.7 = bf16[192,96]{1,0:T(8,128)(2,1)S(1)} all-reduce(f32[192,96]{1,0:T(8,128)S(1)} %fusion.20), channel_id=1, replica_groups=mesh['dp'=8,'mp'=4] {'mp'}, use_global_device_ids=true, to_apply=%region_4.5 | all-reduce | flops 18432 | bytes 110592 | tf_op jit(solution)/shard_map/psum | solution.py:52
  88.8 0.0 copy-done.1
  88.8 0.2 fusion.21
  89.0 25.9 %fusion = f32[16,896]{1,0:T(8,128)S(1)} fusion(f32[96,896]{1,0:T(8,128)S(1)} %fusion.21), kind=kCustom, calls=%all-reduce-scatter | all-reduce-scatter fusion | flops 114689 | bytes 401920
  114.9 2.4 %collective-permute-start = (f32[16,896]{1,0:T(8,128)S(1)}, f32[16,896]{1,0:T(8,128)S(1)}, u32[]{:S(2)}, u32[]{:S(2)}) collective-permute-start(f32[16,896]{1,0:T(8,128)S(1)} %fusion), channel_id=1, source_target_pairs={{0,4},{4,8},{8,12},{12,16},{16,20},{20,24},{24,28},{1,5},{5,9},{9,... | collective-permute-start | bytes 172040
  117.3 3.2 %collective-permute-start.1 = (f32[12,896]{1,0:T(8,128)S(1)}, f32[12,896]{1,0:T(8,128)S(1)}, u32[]{:S(2)}, u32[]{:S(2)}) collective-permute-start(f32[12,896]{1,0:T(8,128)S(1)} %slice), channel_id=1, source_target_pairs={{0,8},{4,12},{8,16},{12,20},{16,24},{20,28},{1,9},{5,13},{9,17},{1... | collective-permute-start | bytes 129032
  120.5 0.0 copy-done.4
  120.5 0.6 fusion.17
  122.4 0.0 collective-permute-done.1
  122.4 0.0 collective-permute-done
  122.4 0.3 concatenate
  122.7 5.7 %all_gather.7 = f32[12,3584]{1,0:T(8,128)S(1)} all-gather(f32[12,896]{1,0:T(8,128)S(1)} %constant_dynamic-slice_fusion), channel_id=1, replica_groups=mesh['dp'=8,'mp'=4] {'mp'}, dimensions={1}, use_global_device_ids=true | all-gather | bytes 215040 | tf_op jit(solution)/shard_map/all_gather | solution.py:78
  128.4 28.2 %all-reduce.5.cloned.1.call-done = f32[2496,96]{0,1:T(8,128)} async-done(((f32[2496,96]{0,1:T(8,128)}), f32[2496,96]{0,1:T(8,128)}) %all-reduce.5.cloned.1.call-update) | async-done | bytes 958480
  156.6 1.7 %dynamic-slice_bitcast_fusion = f32[1,312,96]{1,2,0:T(8,128)} fusion(f32[2496,96]{0,1:T(8,128)} %all-reduce.5.cloned.1.call-done, u32[]{:T(128)S(6)} %multiply.1), kind=kLoop, calls=%fused_computation.18 | loop fusion | bytes 239620 | tf_op jit(solution)/shard_map/broadcast_in_dim | solution.py:89
  158.3 0.7 copy.21
  (7 shorter events, 0.1 us)
Async XLA Ops:
  7.2 50.7 %copy-start = (bf16[96,3584]{1,0:T(8,128)(2,1)S(1)}, bf16[96,3584]{1,0:T(8,128)(2,1)}, u32[]{:S(2)}) copy-start(bf16[96,3584]{1,0:T(8,128)(2,1)} %param.12) | copy-start | bytes 2064388
  9.6 13.7 %all-to-all-start = ((bf16[8,3,1]{1,2,0:T(2,128)(2,1)}), bf16[8,3,1]{1,2,0:T(2,128)(2,1)S(1)}, u32[]{:S(2)}, u32[]{:S(2)}) async-start(bf16[8,3,1]{1,2,0:T(2,128)(2,1)} %convert_element_type.87), calls=%async_computation | async-start | bytes 8192 | tf_op jit(solution)/shard_map/all_to_all | solution.py:35
  23.3 15.3 %all-to-all-start.1 = ((bf16[8,3,7168]{2,1,0:T(4,128)(2,1)}), bf16[8,3,7168]{2,1,0:T(4,128)(2,1)S(1)}, u32[]{:S(2)}, u32[]{:S(2)}) async-start(bf16[8,3,7168]{2,1,0:T(4,128)(2,1)} %all_to_all.13), calls=%async_computation.1 | async-start | bytes 917504 | tf_op jit(solution)/shard_map/all_to_all | solution.py:34
  26.8 31.1 %all-gather.2.cloned.1.call-start = ((), (), s32[]{:S(2)}) async-start(), calls=%async_computation.2 | async-start | bytes 1720320 | tf_op jit(solution)/shard_map/all_gather | solution.py:45
  40.1 116.5 %all-reduce.5.cloned.1.call-start = ((), (), s32[]{:S(2)}) async-start(), calls=%async_computation.3 | async-start | bytes 1966080
  57.9 2.0 %copy-start.2 = (bf16[192,3584]{1,0:T(8,128)(2,1)S(1)}, bf16[192,3584]{1,0:T(8,128)(2,1)}, u32[]{:S(2)}) copy-start(bf16[192,3584]{1,0:T(8,128)(2,1)} %all-gather.2.cloned.1.call-done) | copy-start | bytes 4128772
  59.8 10.8 %copy-start.3 = (bf16[2496,96]{0,1:T(8,128)(2,1)S(1)}, bf16[2496,96]{0,1:T(8,128)(2,1)}, u32[]{:S(2)}) copy-start(bf16[2496,96]{0,1:T(8,128)(2,1)} %param.11) | copy-start | bytes 1437700
  75.4 13.4 %copy-start.1 = (bf16[192,896]{1,0:T(8,128)(2,1)S(1)}, bf16[192,896]{1,0:T(8,128)(2,1)}, u32[]{:S(2)}) copy-start(bf16[192,896]{1,0:T(8,128)(2,1)} %reshape.78) | copy-start | bytes 1032196
  76.7 43.8 %copy-start.4 = (u32[32]{0:T(128)S(1)}, u32[32]{0:T(128)}, u32[]{:S(2)}) copy-start(u32[32]{0:T(128)} %constant.17) | copy-start | bytes 388
  114.9 7.5 %collective-permute-start = (f32[16,896]{1,0:T(8,128)S(1)}, f32[16,896]{1,0:T(8,128)S(1)}, u32[]{:S(2)}, u32[]{:S(2)}) collective-permute-start(f32[16,896]{1,0:T(8,128)S(1)} %fusion), channel_id=1, source_target_pairs={{0,4},{4,8},{8,12},{12,16},{16,20},{20,24},{24,28},{1,5},{5,9},{9,... | collective-permute-start | bytes 172040
  117.3 5.1 %collective-permute-start.1 = (f32[12,896]{1,0:T(8,128)S(1)}, f32[12,896]{1,0:T(8,128)S(1)}, u32[]{:S(2)}, u32[]{:S(2)}) collective-permute-start(f32[12,896]{1,0:T(8,128)S(1)} %slice), channel_id=1, source_target_pairs={{0,8},{4,12},{8,16},{12,20},{16,24},{20,28},{1,9},{5,13},{9,17},{1... | collective-permute-start | bytes 129032
Sparse Core Ops, SparseCore 0:
  40.2 17.5 all-gather.1
  76.9 79.7 all-reduce.4
where the time goes:
time: 166 us
  waiting for transfers between devices  61.4 us (37%)
  blocking collectives  43.2 us (26%)
  matrix products  19.9 us (12%)
  starting transfers between devices  16.4 us (10%)
  between operations  15.5 us (9%)
  local copies, waits for them, and re-layouts  7.48 us (5%)
  other arithmetic  1.9 us (1%)
    unnamed x5, waiting for transfers between devices  28.2 us
    unnamed x1, blocking collectives  25.9 us
    all_gather x1, waiting for transfers between devices, body(): feature_rows = lax.all_gather(packed_tokens, 'mp', axis=1, tiled=True)  17.7 us
    psum x1, blocking collectives, body(): low_rank_rows = lax.psum(low_rank_piece, 'mp').astype(jnp.bfloat16)  11.6 us
    all_to_all x1, waiting for transfers between devices, body(): lax.all_to_all(outgoing, 'dp', split_axis=0, concat_axis=0, tiled=True)  11.4 us
    dot_general x1, matrix products, body(): lax.dot_general(feature_rows, down_weight, (((1,), (1,)), ((), ())), pref...  10.8 us
    all_to_all x1, starting transfers between devices, body(): lax.all_to_all(filled, 'dp', split_axis=0, concat_axis=0, tiled=True)  7.31 us
    all_gather x1, blocking collectives, body(): grad_b_rows = lax.all_gather(part_rows, 'mp', axis=1, tiled=True)  5.69 us
  transfers between devices with their start and end apart: 6, of which 4 were waited for; matrix products, arithmetic and copies ran while one was open for 18% of the time, Pallas kernels for 0%

commit v1 on v0

--- a/solution.py
+++ b/solution.py
@@ -1,10 +1,459 @@
+import functools
+
 import jax
 import jax.numpy as jnp
 from jax import lax
+from jax.experimental import pallas as pl
+from jax.experimental.pallas import tpu as pltpu
 from jax.sharding import PartitionSpec as P
 
 
-def body(
+F32 = jnp.float32
+BF16 = jnp.bfloat16
+LANES = 128
+SUB = 8
+NT = (((1,), (1,)), ((), ()))
+TN = (((0,), (0,)), ((), ()))
+
+
+def dot(a, b, dims):
+    return lax.dot_general(a, b, dims, preferred_element_type=F32)
+
+
+def sspec():
+    return pl.BlockSpec(memory_space=pltpu.SMEM)
+
+
+def layout_of(rank, per, brows, width):
+    full, rem = per // LANES, per % LANES
+    half = 0 < rem <= LANES // 2 and rank % (2 * SUB) == 0
+    a_rows = rank * full + (0 if rem == 0 else rank // 2 if half else rank)
+    q, r = brows // SUB, brows % SUB
+    blocks = width // LANES
+    share = SUB // r if r else 1
+    b_rows = blocks * q * SUB + (-(-blocks // share) * SUB if r else 0)
+    return full, rem, half, a_rows, q, r, blocks, share, b_rows
+
+
+ON_CHIP_KIB = 65472
+ROOM = 12500
+
+
+def full(array):
+    zeros = (0,) * len(array.shape)
+    return pl.BlockSpec(array.shape, lambda: zeros)
+
+
+def far_off():
+    return pl.BlockSpec(memory_space=pltpu.HBM)
+
+
+def call(kernel, outs, smem=(), hbm=(), args=(), flops=0, scratch=(), room=48000, hbm_outs=0):
+    nbytes = sum(a.size * a.dtype.itemsize for a in (*hbm, *args, *outs))
+    got = pl.pallas_call(
+        kernel,
+        out_shape=list(outs),
+        in_specs=[sspec() for _ in smem] + [far_off() for _ in hbm] + [full(a) for a in args],
+        out_specs=[far_off() if at < hbm_outs else full(a) for at, a in enumerate(outs)],
+        scratch_shapes=list(scratch),
+        cost_estimate=pl.CostEstimate(flops=flops, bytes_accessed=nbytes, transcendentals=0),
+        compiler_params=pltpu.CompilerParams(vmem_limit_bytes=(ON_CHIP_KIB - room) * 2**10),
+    )(*smem, *hbm, *args)
+    return got[0] if len(outs) == 1 else got
+
+
+def fetch(pairs, sems):
+    copies = [pltpu.make_async_copy(a, b, sems.at[i]) for i, (a, b) in enumerate(pairs)]
+    for copy in copies:
+        copy.start()
+    return copies
+
+
+def pack_kernel(capacity, plan_ref, blocks_ref, out_ref, blocks, plan, counts, sems):
+    owned = blocks_ref.shape[0]
+    loads = fetch([(plan_ref, plan), (blocks_ref, blocks)], sems)
+    for owner in range(owned // capacity):
+        counts[owner] = 0
+    for load in loads:
+        load.wait()
+    copies = []
+    for block in range(owned):
+        owner = plan[block]
+        rank = counts[owner]
+        counts[owner] = rank + 1
+        copies += fetch([(blocks.at[block], out_ref.at[owner * capacity + rank])], sems.at[pl.ds(2 + block, 1)])
+    for copy in copies:
+        copy.wait()
+
+
+def act_kernel(groups, me_ref, gate_ref, up_ref, first_ref, second_ref, padded_ref, low_ref, mine_ref, hidden):
+    rows, width = gate_ref.shape
+    per = width // groups
+    step = 16
+    mine_ref[...] = second_ref[:, columns(me_ref, 0, mine_ref.shape[1])]
+
+    def one(index, carry):
+        at = pl.ds(pl.multiple_of(index * step, step), step)
+        gate_vals = gate_ref[at, :].astype(F32)
+        silu = gate_vals * jax.nn.sigmoid(gate_vals)
+        hidden[at, :] = (silu * up_ref[at, :].astype(F32)).astype(BF16)
+        return carry
+
+    lax.fori_loop(0, rows // step, one, 0)
+    room = padded_ref.shape[2]
+    for group in range(groups):
+        padded_ref[group, :, pl.ds(0, per)] = hidden[:, group * per : (group + 1) * per]
+        if room > per:
+            padded_ref[group, :, pl.ds(per, room - per)] = jnp.zeros((rows, room - per), BF16)
+    low_ref[...] = dot(hidden[...], first_ref[...], NT)
+
+
+def shaped(shape, dtype):
+    return jax.ShapeDtypeStruct(shape, dtype)
+
+
+def columns(me, bit, width):
+    return pl.ds(pl.multiple_of((me[0] ^ bit) * width, LANES), width)
+
+
+def through_kernel(own_ref, second_ref, out_ref):
+    out_ref[...] = dot(own_ref[...], second_ref[...], NT).astype(BF16)
+
+
+def add_kernel(one_ref, other_ref, out_ref):
+    out_ref[...] = one_ref[...] + other_ref[...]
+
+
+def make_share(groups, brows, width, rank, per):
+    _, _, _, _, q, r, blocks, share, _ = layout_of(rank, per, brows, width)
+
+    def kernel(here_ref, x_ref, low_a, low_b, out_ref, prod):
+        low = (low_a[...] + low_b[...]).astype(BF16)
+        prod[...] = dot(low, x_ref[...], TN)
+        for group in range(groups):
+            at = 0
+            for j in range(blocks):
+                for k in range(q):
+                    out_ref[group, pl.ds(at, SUB), :] = prod[
+                        pl.ds(group * brows + k * SUB, SUB), pl.ds(j * LANES, LANES)
+                    ].astype(BF16)
+                    at += SUB
+            if r:
+                for j in range(0, blocks, share):
+                    pieces = [
+                        prod[pl.ds(group * brows + q * SUB, r), pl.ds(i * LANES, LANES)]
+                        for i in range(j, min(j + share, blocks))
+                    ]
+                    lack = SUB - r * len(pieces)
+                    if lack:
+                        pieces.append(jnp.zeros((lack, LANES), F32))
+                    out_ref[group, pl.ds(at, SUB), :] = jnp.concatenate(pieces, 0).astype(BF16)
+                    at += SUB
+
+    return kernel
+
+
+def make_send(groups, brows, width, rank, per):
+    full_, rem, half, a_rows, _, _, _, _, b_rows = layout_of(rank, per, brows, width)
+
+    def kernel(here_ref, part_0, part_1, part_2, part_3, padded_ref, share_ref, through_ref, *outs):
+        parts = [part[...].astype(F32) for part in (part_0, part_1, part_2, part_3)]
+        through = ((parts[0] + parts[1]) + (parts[2] + parts[3])).astype(BF16)
+        through_ref[...] = through
+        for peer, out_ref in enumerate(outs):
+            for side in range(2):
+                group = here_ref[0] ^ (peer + side * len(outs))
+                piece = dot(through, padded_ref[group], TN)
+                for j in range(full_):
+                    out_ref[side, pl.ds(j * rank, rank), :] = piece[:, j * LANES : (j + 1) * LANES].astype(BF16)
+                if rem:
+                    last = piece[:, full_ * LANES : (full_ + 1) * LANES]
+                    if half:
+                        last = last[: rank // 2] + pltpu.roll(last[rank // 2 :], LANES // 2, 1)
+                    out_ref[side, pl.ds(full_ * rank, last.shape[0]), :] = last.astype(BF16)
+                out_ref[side, pl.ds(a_rows, b_rows), :] = share_ref[group]
+
+    return kernel
+
+
+def half_kernel(*refs):
+    *parts, mine_ref, other_ref = refs
+    for side in range(2):
+        total = parts[0][side].astype(F32)
+        for part in parts[1:]:
+            total = total + part[side].astype(F32)
+        if side:
+            other_ref[...] = total.astype(BF16)
+        else:
+            mine_ref[...] = total
+
+
+def make_sum_b(groups, brows, width, rank, per):
+    _, _, _, a_rows, _, _, _, _, b_rows = layout_of(rank, per, brows, width)
+
+    def kernel(mine_ref, other_ref, out_ref):
+        at = pl.ds(a_rows, b_rows)
+        out_ref[...] = mine_ref[at] + other_ref[at].astype(F32)
+
+    return kernel
+
+
+def make_sum_a(groups, brows, width, rank, per):
+    full_, rem, half, a_rows, *_ = layout_of(rank, per, brows, width)
+
+    def kernel(mine_ref, other_ref, a_ref, total):
+        at = pl.ds(0, a_rows)
+        total[...] = mine_ref[at] + other_ref[at].astype(F32)
+        for j in range(full_):
+            a_ref[0, :, pl.ds(j * LANES, LANES)] = total[pl.ds(j * rank, rank), :]
+        if rem:
+            at = pl.ds(full_ * LANES, rem)
+            if half:
+                last = total[pl.ds(full_ * rank, rank // 2), :]
+                a_ref[0, pl.ds(0, rank // 2), at] = last[:, :rem]
+                a_ref[0, pl.ds(rank // 2, rank // 2), at] = pltpu.roll(last, LANES // 2, 1)[:, :rem]
+            else:
+                a_ref[0, :, at] = total[pl.ds(full_ * rank, rank), :][:, :rem]
+
+    return kernel
+
+
+def make_join(groups, brows, width, rank, per):
+    _, _, _, _, q, r, blocks, share, _ = layout_of(rank, per, brows, width)
+
+    def kernel(me_ref, own_ref, core_ref, x_ref, far_ref, out_ref):
+        for bit, ref in enumerate((own_ref, core_ref, x_ref, far_ref)):
+            base = (me_ref[0] ^ bit) * width
+            at = 0
+            for j in range(blocks):
+                cols = pl.ds(pl.multiple_of(base + j * LANES, LANES), LANES)
+                for k in range(q):
+                    out_ref[pl.ds(k * SUB, SUB), cols] = ref[pl.ds(at, SUB), :]
+                    at += SUB
+            if r:
+                for j in range(0, blocks, share):
+                    for i in range(j, min(j + share, blocks)):
+                        cols = pl.ds(pl.multiple_of(base + i * LANES, LANES), LANES)
+                        out_ref[pl.ds(q * SUB, r), cols] = ref[pl.ds(at + (i - j) * r, r), :]
+                    at += SUB
+
+    return kernel
+
+
+def near_kernel(
+    tile, me_ref, first_ref, weight_ref, own_ref, core_ref, through_ref, out_ref, first, weight, total, arrive, leave
+):
+    hid = weight_ref.shape[0]
+    width = own_ref.shape[1]
+    spans = [pl.ds(at, min(tile, hid - at)) for at in range(0, hid, tile)]
+    coming = fetch([(weight_ref.at[:, columns(me_ref, bit, width)], weight.at[bit]) for bit in range(2)], arrive)
+    small = fetch([(first_ref, first)], arrive.at[pl.ds(2, 1)])
+    small[0].wait()
+    for span in spans:
+        total[:, span] = dot(through_ref[...], first[:, span], (((1,), (0,)), ((), ())))
+    leaving = []
+    for bit, ref in enumerate((own_ref, core_ref)):
+        coming[bit].wait()
+        for index, span in enumerate(spans):
+            total[:, span] += dot(ref[...], weight[bit, span], NT)
+            if bit:
+                leaving += fetch([(total.at[:, span], out_ref.at[:, span])], leave.at[pl.ds(index, 1)])
+    for copy in leaving:
+        copy.wait()
+
+
+def distant_kernel(
+    tile, me_ref, weight_ref, total_ref, gate_in, up_in, x_ref, far_ref, gate_ref, up_ref,
+    weight, total, gate, up, grad_gate, grad_up, arrive, leave,
+):
+    hid = weight_ref.shape[0]
+    width = x_ref.shape[1]
+    spans = [pl.ds(at, min(tile, hid - at)) for at in range(0, hid, tile)]
+    coming = fetch(
+        [
+            (weight_ref.at[:, columns(me_ref, 2, width)], weight.at[0]),
+            (total_ref, total),
+            (weight_ref.at[:, columns(me_ref, 3, width)], weight.at[1]),
+            (gate_in, gate),
+            (up_in, up),
+        ],
+        arrive,
+    )
+    leaving = []
+    coming[0].wait()
+    coming[1].wait()
+    for span in spans:
+        total[:, span] += dot(x_ref[...], weight[0, span], NT)
+    for copy in coming[2:]:
+        copy.wait()
+    for index, span in enumerate(spans):
+        acc = total[:, span] + dot(far_ref[...], weight[1, span], NT)
+        gate_vals = gate[:, span].astype(F32)
+        sig = jax.nn.sigmoid(gate_vals)
+        slope = up[:, span].astype(F32) * sig * (1.0 + gate_vals * (1.0 - sig))
+        grad_gate[:, span] = (acc * slope).astype(BF16)
+        grad_up[:, span] = (acc * (gate_vals * sig)).astype(BF16)
+        leaving += fetch([(grad_gate.at[:, span], gate_ref.at[:, span]), (grad_up.at[:, span], up_ref.at[:, span])], leave.at[index])
+    for copy in leaving:
+        copy.wait()
+
+
+def near_call(me, own, core, through, first_t, weight, tile=512):
+    rows, width = own.shape
+    hid = weight.shape[0]
+    rank = through.shape[1]
+    return call(
+        functools.partial(near_kernel, tile),
+        [shaped((rows, hid), F32)],
+        [me],
+        [first_t, weight],
+        [own, core, through],
+        flops=4 * rows * hid * width,
+        scratch=[
+            pltpu.VMEM((rank, hid), BF16),
+            pltpu.VMEM((2, hid, width), BF16),
+            pltpu.VMEM((rows, hid), F32),
+            pltpu.SemaphoreType.DMA((3,)),
+            pltpu.SemaphoreType.DMA((-(-hid // tile),)),
+        ],
+        room=ROOM,
+        hbm_outs=1,
+    )
+
+
+def distant_call(me, total, other, far, weight, gate, up, tile=512):
+    rows, width = other.shape
+    hid = weight.shape[0]
+    return call(
+        functools.partial(distant_kernel, tile),
+        [shaped((rows, hid), BF16)] * 2,
+        [me],
+        [weight, total, gate, up],
+        [other, far],
+        flops=4 * rows * hid * width,
+        scratch=[
+            pltpu.VMEM((2, hid, width), BF16),
+            pltpu.VMEM((rows, hid), F32),
+            *[pltpu.VMEM((rows, hid), BF16)] * 4,
+            pltpu.SemaphoreType.DMA((5,)),
+            pltpu.SemaphoreType.DMA((-(-hid // tile), 2)),
+        ],
+        room=ROOM,
+        hbm_outs=2,
+    )
+
+
+def swap(value, bit):
+    count = lax.axis_size("mp")
+    return lax.ppermute(value, "mp", [(i, i ^ bit) for i in range(count)])
+
+
+def trade(value, bit):
+    count = lax.axis_size("dp")
+    return lax.ppermute(value, "dp", [(i, i ^ bit) for i in range(count)])
+
+
+def fast_body(*args):
+    return fast_layer(*args)
+
+
+def fast_layer(output_gradient, gate_preactivation, up_preactivation, down_weight, adapter_first, adapter_second, plan):
+    groups = lax.axis_size("dp")
+    owned = plan.shape[0]
+    capacity = owned // groups
+    tokens, width = output_gradient.shape
+    hid, rank = adapter_first.shape
+    per, brows = hid // groups, rank // groups
+    tall = tokens // owned
+    me = lax.axis_index("mp").astype(jnp.int32).reshape(1)
+    here = lax.axis_index("dp").astype(jnp.int32).reshape(1)
+    first_t = adapter_first.T
+    room = -(-per // LANES) * LANES
+    _, _, _, a_rows, _, _, _, _, b_rows = layout_of(rank, per, brows, width)
+    sizes = (groups, brows, width, rank, per)
+
+    outgoing = call(
+        functools.partial(pack_kernel, capacity),
+        [shaped((owned, tall, width), BF16)],
+        hbm=[plan, output_gradient.reshape(owned, tall, width)],
+        scratch=[
+            pltpu.VMEM((owned, tall, width), BF16),
+            pltpu.SMEM((owned,), jnp.int32),
+            pltpu.SMEM((groups,), jnp.int32),
+            pltpu.SemaphoreType.DMA((owned + 2,)),
+        ],
+        room=0,
+        hbm_outs=1,
+    )
+    packed = lax.all_to_all(outgoing, "dp", split_axis=0, concat_axis=0, tiled=True).reshape(tokens, width)
+
+    padded, low_0, second = call(
+        functools.partial(act_kernel, groups),
+        [
+            shaped((groups, tokens, room), BF16),
+            shaped((tokens, rank), F32),
+            shaped((rank, width), BF16),
+        ],
+        [me],
+        args=[gate_preactivation, up_preactivation, first_t, adapter_second],
+        flops=2 * tokens * hid * rank,
+        scratch=[pltpu.VMEM((tokens, hid), BF16)],
+    )
+    low_1 = swap(low_0, 1)
+    low_a = call(add_kernel, [shaped((tokens, rank), F32)], args=[low_0, low_1])
+    low_b = swap(low_a, 2)
+
+    part_0 = call(
+        through_kernel, [shaped((tokens, rank), BF16)], args=[packed, second], flops=2 * tokens * width * rank
+    )
+    part_2 = swap(part_0, 2)
+    part_3 = swap(part_0, 3)
+    part_1 = swap(part_0, 1)
+    share = call(
+        make_share(*sizes),
+        [shaped((groups, b_rows, LANES), BF16)],
+        [here],
+        args=[packed, low_a, low_b],
+        scratch=[pltpu.VMEM((rank, width), F32)],
+    )
+    side = swap(packed, 2)
+    core = swap(packed, 1)
+
+    peers = groups // 2
+    through, *payload = call(
+        make_send(*sizes),
+        [shaped((tokens, rank), BF16)] + [shaped((2, a_rows + b_rows, LANES), BF16)] * peers,
+        [here],
+        args=[part_0, part_1, part_2, part_3, padded, share],
+        flops=2 * tokens * hid * rank,
+    )
+    arrived = [payload[0]]
+    for peer in range(1, peers):
+        arrived.append(trade(payload[peer], peer))
+
+    total = near_call(me, packed, core, through, first_t, down_weight)
+    far = swap(side, 1)
+    mine, other = call(
+        half_kernel, [shaped((a_rows + b_rows, LANES), F32), shaped((a_rows + b_rows, LANES), BF16)], args=arrived
+    )
+    landed = trade(other, peers)
+    grad_gate, grad_up = distant_call(me, total, side, far, down_weight, gate_preactivation, up_preactivation)
+
+    b_0 = call(make_sum_b(*sizes), [shaped((b_rows, LANES), F32)], args=[mine, landed])
+    b_3 = swap(b_0, 3)
+    b_2 = swap(b_0, 2)
+    b_1 = swap(b_0, 1)
+    grad_a_t = call(
+        make_sum_a(*sizes),
+        [shaped((1, rank, per), F32)],
+        args=[mine, landed],
+        scratch=[pltpu.VMEM((a_rows, LANES), F32)],
+    )
+    grad_b = call(make_join(*sizes), [shaped((brows, 4 * width), F32)], [me], args=[b_0, b_1, b_2, b_3])
+    return grad_gate, grad_up, jnp.swapaxes(grad_a_t, 1, 2), grad_b
+
+
+def general_body(
     output_gradient,
     gate_preactivation,
     up_preactivation,
@@ -89,19 +538,44 @@
     return (grad_gate, grad_up, grad_a_rows[None], grad_b_rows)
 
 
+def fits(mesh, args):
+    groups, parts = mesh.shape["dp"], mesh.shape["mp"]
+    gradient, _, _, _, first, _, plan = args
+    owned = plan.shape[0] // groups
+    tokens, width = gradient.shape[0] // groups, gradient.shape[1] // parts
+    hid, rank = first.shape[0] // parts, first.shape[1]
+    return (
+        parts == 4
+        and groups > 4 and groups & (groups - 1) == 0
+        and owned % groups == 0
+        and tokens == owned * SUB
+        and tokens % 16 == 0
+        and width % LANES == 0
+        and hid % groups == 0
+        and rank % groups == 0
+        and rank % (2 * SUB) == 0
+        and SUB % max(rank // groups % SUB, 1) == 0
+    )
+
+
 def solution(mesh):
-    return jax.shard_map(
-        body,
-        mesh=mesh,
-        in_specs=(
-            P("dp", "mp"),
-            P("dp", "mp"),
-            P("dp", "mp"),
-            P("mp", None),
-            P("mp", None),
-            P(),
-            P("dp"),
-        ),
-        out_specs=(P("dp", "mp"), P("dp", "mp"), P("mp", "dp", None), P("dp", None)),
-        check_vma=False,
-    )
+    def step(*args):
+        fast = fits(mesh, args)
+        run = jax.shard_map(
+            fast_body if fast else general_body,
+            mesh=mesh,
+            in_specs=(
+                P("dp", "mp"),
+                P("dp", "mp"),
+                P("dp", "mp"),
+                P("mp", None),
+                P("mp", None),
+                P(),
+                P("dp"),
+            ),
+            out_specs=(P("dp", "mp"), P("dp", "mp"), P("mp", "dp", None), P("dp", None)),
+            check_vma=False,
+        )
+        return run(*args)
+
+    return step

time: 166 us -> 73.8 us (0.44)
  waiting for transfers between devices: 61.4 us -> 19.9 us
  blocking collectives: 43.2 us -> 18.5 us
  matrix products: 19.9 us -> 0 us
  Pallas kernels: 0 us -> 19.1 us
  between operations: 15.5 us -> 0.74 us
  starting transfers between devices: 16.4 us -> 10.6 us
  local copies, waits for them, and re-layouts: 7.48 us -> 4.54 us
  other arithmetic: 1.9 us -> 0 us
    unnamed x5 -> x0, waiting for transfers between devices: 28.2 us -> none
    unnamed x1 -> x0, blocking collectives: 25.9 us -> none
    dot_general x8 -> x0, matrix products: 19.9 us -> none  [the longest x1 10.8 us: body(): lax.dot_general(feature_rows, down_weight, (((1,), (1,)), ((), ())), pref...]
    ppermute x0 -> x15, waiting for transfers between devices: none -> 19.9 us  [the longest x4 13.1 us: trade(): return lax.ppermute(value, 'dp', [(i, i ^ bit) for i in range(count)])]
    pallas_call x0 -> x12, Pallas kernels: none -> 19.1 us  [call(): pl.pallas_call(kernel, out_shape=list(outs), in_specs=[sspec() for _ in s...]
    all_to_all x0 -> x1, blocking collectives: none -> 18.5 us  [fast_layer(): lax.all_to_all(outgoing, 'dp', split_axis=0, concat_axis=0, tiled=True)]
    all_gather x1 -> x0, waiting for transfers between devices: 17.7 us -> none  [body(): feature_rows = lax.all_gather(packed_tokens, 'mp', axis=1, tiled=True)]
    all_to_all x2 -> x0, waiting for transfers between devices: 15.5 us -> none  [the longest x1 11.4 us: body(): lax.all_to_all(outgoing, 'dp', split_axis=0, concat_axis=0, tiled=True)]
  transfers between devices with their start and end apart: 6 -> 15, of which waited for: 4 -> 9; matrix products, arithmetic and copies ran while one was open for 18% -> 0% of each run, Pallas kernels for 0% -> 14%
where the time goes in v1:
time: 73.8 us; the launch traced here: 73.3 us
  waiting for transfers between devices  19.9 us (27%)
  Pallas kernels  19.1 us (26%)
  blocking collectives  18.5 us (25%)
  starting transfers between devices  10.6 us (14%)
  local copies, waits for them, and re-layouts  4.54 us (6%)
  between operations  0.74 us (1%)
    pallas_call x12, Pallas kernels, call(): pl.pallas_call(kernel, out_shape=list(outs), in_specs=[sspec() for _ in s...  19.1 us
    all_to_all x1, blocking collectives, fast_layer(): lax.all_to_all(outgoing, 'dp', split_axis=0, concat_axis=0, tiled=True)  18.5 us
    ppermute x4, waiting for transfers between devices, trade(): return lax.ppermute(value, 'dp', [(i, i ^ bit) for i in range(count)])  13.1 us
    ppermute x11, waiting for transfers between devices, swap(): return lax.ppermute(value, 'mp', [(i, i ^ bit) for i in range(count)])  6.81 us
    ppermute x11, starting transfers between devices, swap(): return lax.ppermute(value, 'mp', [(i, i ^ bit) for i in range(count)])  6.23 us
    unnamed x12, local copies, waits for them, and re-layouts  4.54 us
    ppermute x4, starting transfers between devices, trade(): return lax.ppermute(value, 'dp', [(i, i ^ bit) for i in range(count)])  4.39 us
  transfers between devices with their start and end apart: 15, of which 9 were waited for; matrix products, arithmetic and copies ran while one was open for 0% of the time, Pallas kernels for 14%

profile of v1, /device:TPU:0, one launch (start us, length us, event | category | flops | bytes accessed | tf_op | source)
XLA Modules:
  0.0 73.3 jit_solution(12990107662007331928)
XLA Ops:
  0.6 1.9 %shard_map.102 = bf16[24,8,896]{2,1,0:T(8,128)(2,1)} custom-call(s32[24]{0:T(128)} %plan_ref.1, bf16[24,8,896]{2,1,0:T(8,128)(2,1)} %bitcast.13), custom_call_target="tpu_custom_call" | custom-call | bytes 688224 | tf_op jit(solution)/shard_map/pallas_call | solution.py:53
  2.5 18.5 %all_to_all.5 = bf16[24,8,896]{2,1,0:T(8,128)(2,1)S(1)} all-to-all(bf16[24,8,896]{2,1,0:T(8,128)(2,1)} %shard_map.102), channel_id=1, replica_groups=mesh['dp'=8,'mp'=4] {'dp'}, dimensions={0} | all-to-all | bytes 688128 | tf_op jit(solution)/shard_map/all_to_all | solution.py:388
  21.1 1.5 %collective-permute-start.6 = (bf16[192,896]{1,0:T(8,128)(2,1)S(1)}, bf16[192,896]{1,0:T(8,128)(2,1)S(1)}, u32[]{:S(2)}, u32[]{:S(2)}) collective-permute-start(bf16[192,896]{1,0:T(8,128)(2,1)S(1)} %bitcast.6), channel_id=1, source_target_pairs={{0,2},{1,3},{2,0},{3,1},{4,6},{5,7},{6,4},{7,5},{8,10},{9,11},{10,... | collective-permute-start | bytes 1032200 | tf_op jit(solution)/shard_map/ppermute | solution.py:348
  22.6 1.2 %copy-done = bf16[192,2496]{1,0:T(8,128)(2,1)S(1)} copy-done((bf16[192,2496]{1,0:T(8,128)(2,1)S(1)}, bf16[192,2496]{1,0:T(8,128)(2,1)}, u32[]{:S(2)}) %copy-start) | copy-done | bytes 958488
  23.8 0.0 copy-start.2
  23.8 1.2 %copy-done.2 = bf16[192,2496]{1,0:T(8,128)(2,1)S(1)} copy-done((bf16[192,2496]{1,0:T(8,128)(2,1)S(1)}, bf16[192,2496]{1,0:T(8,128)(2,1)}, u32[]{:S(2)}) %copy-start.2) | copy-done | bytes 958488
  25.0 1.0 %copy-done.3 = bf16[2496,96]{0,1:T(8,128)(2,1)S(1)} copy-done((bf16[2496,96]{0,1:T(8,128)(2,1)S(1)}, bf16[2496,96]{0,1:T(8,128)(2,1)}, u32[]{:S(2)}) %copy-start.3) | copy-done | bytes 479256
  26.0 1.1 %copy-done.5 = bf16[96,3584]{1,0:T(8,128)(2,1)S(1)} copy-done((bf16[96,3584]{1,0:T(8,128)(2,1)S(1)}, bf16[96,3584]{1,0:T(8,128)(2,1)}, u32[]{:S(2)}) %copy-start.5) | copy-done | bytes 688152
  27.1 1.0 %shard_map.103 = (bf16[8,192,384]{2,1,0:T(8,128)(2,1)S(1)}, f32[192,96]{1,0:T(8,128)S(1)}, bf16[96,896]{1,0:T(8,128)(2,1)S(1)}) custom-call(s32[1]{0:T(128)} %bitcast.me_ref, bf16[192,2496]{1,0:T(8,128)(2,1)S(1)} %copy-done, bf16[192,2496]{1,0:T(8,128)(2,1)S(1)} %copy-done.2, bf16[96,2496]{1,0:T(8,128)(2,1)S(1)} %bitcast.11, bf16[96,3584]{1,0:T(8,128)(2,1)S(1)} %copy-done.5), custom_call_target="tpu_custom_call" | custom-call | flops 92012544 | bytes 4509696 | tf_op jit(solution)/shard_map/pallas_call | solution.py:53
  28.1 0.1 collective-permute-start.4
  28.2 1.3 %collective-permute-done.4.other_ref = f32[192,96]{1,0:T(8,128)S(1)} collective-permute-done((f32[192,96]{1,0:T(8,128)S(1)}, f32[192,96]{1,0:T(8,128)S(1)}, u32[]{:S(2)}, u32[]{:S(2)}) %collective-permute-start.4) | collective-permute-done | bytes 73760 | tf_op jit(solution)/shard_map/ppermute | solution.py:348
  29.5 0.6 collective-permute-start.5
  30.1 0.0 collective-permute-start
  30.1 0.3 shard_map.104.part_0
  30.3 1.7 %collective-permute-start.3 = (bf16[192,96]{1,0:T(8,128)(2,1)S(1)}, bf16[192,96]{1,0:T(8,128)(2,1)S(1)}, u32[]{:S(2)}, u32[]{:S(2)}) collective-permute-start(bf16[192,96]{1,0:T(8,128)(2,1)S(1)} %shard_map.104.part_0), channel_id=1, source_target_pairs={{0,3},{1,2},{2,1},{3,0},{4,7},{5,6},{6,5},{7,4},{8,11},{9,10},{10,... | collective-permute-start | bytes 110600 | tf_op jit(solution)/shard_map/ppermute | solution.py:348
  32.0 0.6 collective-permute-start.2
  32.6 2.6 %collective-permute-done.5.low_b = f32[192,96]{1,0:T(8,128)S(1)} collective-permute-done((f32[192,96]{1,0:T(8,128)S(1)}, f32[192,96]{1,0:T(8,128)S(1)}, u32[]{:S(2)}, u32[]{:S(2)}) %collective-permute-start.5) | collective-permute-done | bytes 73760 | tf_op jit(solution)/shard_map/ppermute | solution.py:348
  35.2 0.0 collective-permute-start.1
  35.2 0.2 shard_map.106.share_ref
  35.5 0.0 collective-permute-done.3.part_3
  35.5 1.0 %collective-permute-done.2.part_2 = bf16[192,96]{1,0:T(8,128)(2,1)S(1)} collective-permute-done((bf16[192,96]{1,0:T(8,128)(2,1)S(1)}, bf16[192,96]{1,0:T(8,128)(2,1)S(1)}, u32[]{:S(2)}, u32[]{:S(2)}) %collective-permute-start.2) | collective-permute-done | bytes 36896 | tf_op jit(solution)/shard_map/ppermute | solution.py:348
  36.5 0.0 collective-permute-done.1.part_1
  36.5 0.5 shard_map.107
  37.0 1.0 %collective-permute-start.8 = (bf16[2,328,128]{2,1,0:T(8,128)(2,1)S(1)}, bf16[2,328,128]{2,1,0:T(8,128)(2,1)S(1)}, u32[]{:S(2)}, u32[]{:S(2)}) collective-permute-start(bf16[2,328,128]{2,1,0:T(8,128)(2,1)S(1)} %get-tuple-element.23), channel_id=1, source_target_pairs={{0,4},{4,0},{8,12},{12,8},{16,20},{20,16},{24,28},{28,24},{1,5},{5... | collective-permute-start | bytes 503816 | tf_op jit(solution)/shard_map/ppermute | solution.py:353
  37.9 0.3 collective-permute-start.9
  38.3 2.3 %collective-permute-start.10 = (bf16[2,328,128]{2,1,0:T(8,128)(2,1)S(1)}, bf16[2,328,128]{2,1,0:T(8,128)(2,1)S(1)}, u32[]{:S(2)}, u32[]{:S(2)}) collective-permute-start(bf16[2,328,128]{2,1,0:T(8,128)(2,1)S(1)} %get-tuple-element.25), channel_id=1, source_target_pairs={{0,12},{4,8},{8,4},{12,0},{16,28},{20,24},{24,20},{28,16},{1,13},{... | collective-permute-start | bytes 503816 | tf_op jit(solution)/shard_map/ppermute | solution.py:353
  40.5 0.0 collective-permute-done.6.x_ref
  40.5 0.0 collective-permute-start.7
  40.5 2.8 %collective-permute-done.8.refs_1_ = bf16[2,328,128]{2,1,0:T(8,128)(2,1)S(1)} collective-permute-done((bf16[2,328,128]{2,1,0:T(8,128)(2,1)S(1)}, bf16[2,328,128]{2,1,0:T(8,128)(2,1)S(1)}, u32[]{:S(2)}, u32[]{:S(2)}) %collective-permute-start.8) | collective-permute-done | bytes 167968 | tf_op jit(solution)/shard_map/ppermute | solution.py:353
  43.3 1.8 %collective-permute-done.9.refs_2_ = bf16[2,328,128]{2,1,0:T(8,128)(2,1)S(1)} collective-permute-done((bf16[2,328,128]{2,1,0:T(8,128)(2,1)S(1)}, bf16[2,328,128]{2,1,0:T(8,128)(2,1)S(1)}, u32[]{:S(2)}, u32[]{:S(2)}) %collective-permute-start.9) | collective-permute-done | bytes 167968 | tf_op jit(solution)/shard_map/ppermute | solution.py:353
  45.1 3.0 %collective-permute-done.10.refs_3_ = bf16[2,328,128]{2,1,0:T(8,128)(2,1)S(1)} collective-permute-done((bf16[2,328,128]{2,1,0:T(8,128)(2,1)S(1)}, bf16[2,328,128]{2,1,0:T(8,128)(2,1)S(1)}, u32[]{:S(2)}, u32[]{:S(2)}) %collective-permute-start.10) | collective-permute-done | bytes 167968 | tf_op jit(solution)/shard_map/ppermute | solution.py:353
  48.1 0.1 shard_map.110
  48.2 0.8 %collective-permute-start.11 = (bf16[328,128]{1,0:T(8,128)(2,1)S(1)}, bf16[328,128]{1,0:T(8,128)(2,1)S(1)}, u32[]{:S(2)}, u32[]{:S(2)}) collective-permute-start(bf16[328,128]{1,0:T(8,128)(2,1)S(1)} %get-tuple-element.27), channel_id=1, source_target_pairs={{0,16},{4,20},{8,24},{12,28},{16,0},{20,4},{24,8},{28,12},{1,17},{... | collective-permute-start | bytes 251912 | tf_op jit(solution)/shard_map/ppermute | solution.py:353
  49.0 5.5 %collective-permute-done.11.other_ref = bf16[328,128]{1,0:T(8,128)(2,1)S(1)} collective-permute-done((bf16[328,128]{1,0:T(8,128)(2,1)S(1)}, bf16[328,128]{1,0:T(8,128)(2,1)S(1)}, u32[]{:S(2)}, u32[]{:S(2)}) %collective-permute-start.11) | collective-permute-done | bytes 84000 | tf_op jit(solution)/shard_map/ppermute | solution.py:353
  54.5 0.0 collective-permute-start.14
  54.5 0.1 collective-permute-start.13
  54.6 1.8 %collective-permute-start.12 = (f32[88,128]{1,0:T(8,128)S(1)}, f32[88,128]{1,0:T(8,128)S(1)}, u32[]{:S(2)}, u32[]{:S(2)}) collective-permute-start(f32[88,128]{1,0:T(8,128)S(1)} %shard_map.112.own_ref), channel_id=1, source_target_pairs={{0,1},{1,0},{2,3},{3,2},{4,5},{5,4},{6,7},{7,6},{8,9},{9,8},{10,11... | collective-permute-start | bytes 135176 | tf_op jit(solution)/shard_map/ppermute | solution.py:348
  56.4 0.7 %shard_map.111 = f32[1,96,312]{2,1,0:T(8,128)} custom-call(f32[328,128]{1,0:T(8,128)S(1)} %get-tuple-element.26.mine_ref, bf16[328,128]{1,0:T(8,128)(2,1)S(1)} %collective-permute-done.11.other_ref), custom_call_target="tpu_custom_call" | custom-call | bytes 371712 | tf_op jit(solution)/shard_map/pallas_call | solution.py:53
  57.1 0.9 %collective-permute-done.14.far_ref = f32[88,128]{1,0:T(8,128)S(1)} collective-permute-done((f32[88,128]{1,0:T(8,128)S(1)}, f32[88,128]{1,0:T(8,128)S(1)}, u32[]{:S(2)}, u32[]{:S(2)}) %collective-permute-start.14) | collective-permute-done | bytes 45088 | tf_op jit(solution)/shard_map/ppermute | solution.py:348
  58.0 1.0 %collective-permute-done.13.x_ref = f32[88,128]{1,0:T(8,128)S(1)} collective-permute-done((f32[88,128]{1,0:T(8,128)S(1)}, f32[88,128]{1,0:T(8,128)S(1)}, u32[]{:S(2)}, u32[]{:S(2)}) %collective-permute-start.13) | collective-permute-done | bytes 45088 | tf_op jit(solution)/shard_map/ppermute | solution.py:348
  59.0 0.0 collective-permute-done.12.core_ref
  59.0 0.7 shard_map.113
  59.7 0.0 collective-permute-done.core_ref
  59.7 0.0 copy-done.4
  59.7 6.5 %shard_map.108.total_ref = f32[192,2496]{1,0:T(8,128)} custom-call(s32[1]{0:T(128)} %bitcast.me_ref, bf16[96,2496]{1,0:T(8,128)(2,1)S(1)} %bitcast.12, bf16[2496,3584]{1,0:T(8,128)(2,1)} %weight_ref.3, bf16[192,896]{1,0:T(8,128)(2,1)S(1)} %bitcast.10, bf16[192,896]{1,0:T(8,128)(2,1)S(1)} %collective-permute-done.core_ref, ...), custom_call_target="tpu_custom_call" | custom-call | flops 1717567488 | bytes 21012480 | tf_op jit(solution)/shard_map/pallas_call | solution.py:53
  66.2 0.0 collective-permute-done.7.far_ref
  66.2 0.0 copy-done.1
  66.2 7.1 %shard_map.109 = (bf16[192,2496]{1,0:T(8,128)(2,1)}, bf16[192,2496]{1,0:T(8,128)(2,1)}) custom-call(s32[1]{0:T(128)} %bitcast.me_ref, bf16[2496,3584]{1,0:T(8,128)(2,1)} %weight_ref.3, f32[192,2496]{1,0:T(8,128)} %shard_map.108.total_ref, bf16[192,2496]{1,0:T(8,128)(2,1)S(1)} %copy-done.1, bf16[192,2496]{1,0:T(8,128)(2,1)} %up_in.1, ...), custom_call_target="tpu_custom_call" | custom-call | flops 1717567488 | bytes 24330240 | tf_op jit(solution)/shard_map/pallas_call | solution.py:53
  (7 shorter events, 0.0 us)
Async XLA Ops:
  21.1 19.5 %collective-permute-start.6 = (bf16[192,896]{1,0:T(8,128)(2,1)S(1)}, bf16[192,896]{1,0:T(8,128)(2,1)S(1)}, u32[]{:S(2)}, u32[]{:S(2)}) collective-permute-start(bf16[192,896]{1,0:T(8,128)(2,1)S(1)} %bitcast.6), channel_id=1, source_target_pairs={{0,2},{1,3},{2,0},{3,1},{4,6},{5,7},{6,4},{7,5},{8,10},{9,11},{10,... | collective-permute-start | bytes 1032200 | tf_op jit(solution)/shard_map/ppermute | solution.py:348
  22.5 1.2 %copy-start = (bf16[192,2496]{1,0:T(8,128)(2,1)S(1)}, bf16[192,2496]{1,0:T(8,128)(2,1)}, u32[]{:S(2)}) copy-start(bf16[192,2496]{1,0:T(8,128)(2,1)} %gate_in.1) | copy-start | bytes 2875396
  23.8 1.2 %copy-start.2 = (bf16[192,2496]{1,0:T(8,128)(2,1)S(1)}, bf16[192,2496]{1,0:T(8,128)(2,1)}, u32[]{:S(2)}) copy-start(bf16[192,2496]{1,0:T(8,128)(2,1)} %up_in.1) | copy-start | bytes 2875396
  25.0 1.0 %copy-start.3 = (bf16[2496,96]{0,1:T(8,128)(2,1)S(1)}, bf16[2496,96]{0,1:T(8,128)(2,1)}, u32[]{:S(2)}) copy-start(bf16[2496,96]{0,1:T(8,128)(2,1)} %param.11) | copy-start | bytes 1437700
  26.0 1.1 %copy-start.5 = (bf16[96,3584]{1,0:T(8,128)(2,1)S(1)}, bf16[96,3584]{1,0:T(8,128)(2,1)}, u32[]{:S(2)}) copy-start(bf16[96,3584]{1,0:T(8,128)(2,1)} %second_ref.1) | copy-start | bytes 2064388
  28.1 1.4 %collective-permute-start.4 = (f32[192,96]{1,0:T(8,128)S(1)}, f32[192,96]{1,0:T(8,128)S(1)}, u32[]{:S(2)}, u32[]{:S(2)}) collective-permute-start(f32[192,96]{1,0:T(8,128)S(1)} %get-tuple-element.18.one_ref), channel_id=1, source_target_pairs={{0,1},{1,0},{2,3},{3,2},{4,5},{5,4},{6,7},{7,6},{8,9},{9,8},{10,11... | collective-permute-start | bytes 221192 | tf_op jit(solution)/shard_map/ppermute | solution.py:348
  29.5 5.7 %collective-permute-start.5 = (f32[192,96]{1,0:T(8,128)S(1)}, f32[192,96]{1,0:T(8,128)S(1)}, u32[]{:S(2)}, u32[]{:S(2)}) collective-permute-start(f32[192,96]{1,0:T(8,128)S(1)} %shard_map.105.low_a), channel_id=1, source_target_pairs={{0,2},{1,3},{2,0},{3,1},{4,6},{5,7},{6,4},{7,5},{8,10},{9,11},{10,... | collective-permute-start | bytes 221192 | tf_op jit(solution)/shard_map/ppermute | solution.py:348
  30.1 29.6 %collective-permute-start = (bf16[192,896]{1,0:T(8,128)(2,1)S(1)}, bf16[192,896]{1,0:T(8,128)(2,1)S(1)}, u32[]{:S(2)}, u32[]{:S(2)}) collective-permute-start(bf16[192,896]{1,0:T(8,128)(2,1)S(1)} %bitcast.7), channel_id=1, source_target_pairs={{0,1},{1,0},{2,3},{3,2},{4,5},{5,4},{6,7},{7,6},{8,9},{9,8},{10,11... | collective-permute-start | bytes 1032200 | tf_op jit(solution)/shard_map/ppermute | solution.py:348
  30.3 5.1 %collective-permute-start.3 = (bf16[192,96]{1,0:T(8,128)(2,1)S(1)}, bf16[192,96]{1,0:T(8,128)(2,1)S(1)}, u32[]{:S(2)}, u32[]{:S(2)}) collective-permute-start(bf16[192,96]{1,0:T(8,128)(2,1)S(1)} %shard_map.104.part_0), channel_id=1, source_target_pairs={{0,3},{1,2},{2,1},{3,0},{4,7},{5,6},{6,5},{7,4},{8,11},{9,10},{10,... | collective-permute-start | bytes 110600 | tf_op jit(solution)/shard_map/ppermute | solution.py:348
  32.0 4.5 %collective-permute-start.2 = (bf16[192,96]{1,0:T(8,128)(2,1)S(1)}, bf16[192,96]{1,0:T(8,128)(2,1)S(1)}, u32[]{:S(2)}, u32[]{:S(2)}) collective-permute-start(bf16[192,96]{1,0:T(8,128)(2,1)S(1)} %shard_map.104.part_0), channel_id=1, source_target_pairs={{0,2},{1,3},{2,0},{3,1},{4,6},{5,7},{6,4},{7,5},{8,10},{9,11},{10,... | collective-permute-start | bytes 110600 | tf_op jit(solution)/shard_map/ppermute | solution.py:348
  35.2 1.3 %collective-permute-start.1 = (bf16[192,96]{1,0:T(8,128)(2,1)S(1)}, bf16[192,96]{1,0:T(8,128)(2,1)S(1)}, u32[]{:S(2)}, u32[]{:S(2)}) collective-permute-start(bf16[192,96]{1,0:T(8,128)(2,1)S(1)} %shard_map.104.part_0), channel_id=1, source_target_pairs={{0,1},{1,0},{2,3},{3,2},{4,5},{5,4},{6,7},{7,6},{8,9},{9,8},{10,11... | collective-permute-start | bytes 110600 | tf_op jit(solution)/shard_map/ppermute | solution.py:348
  35.2 24.5 %copy-start.4 = (bf16[2496,96]{0,1:T(8,128)(2,1)S(1)}, bf16[2496,96]{0,1:T(8,128)(2,1)}, u32[]{:S(2)}) copy-start(bf16[2496,96]{0,1:T(8,128)(2,1)} %param.11) | copy-start | bytes 1437700
  37.0 6.3 %collective-permute-start.8 = (bf16[2,328,128]{2,1,0:T(8,128)(2,1)S(1)}, bf16[2,328,128]{2,1,0:T(8,128)(2,1)S(1)}, u32[]{:S(2)}, u32[]{:S(2)}) collective-permute-start(bf16[2,328,128]{2,1,0:T(8,128)(2,1)S(1)} %get-tuple-element.23), channel_id=1, source_target_pairs={{0,4},{4,0},{8,12},{12,8},{16,20},{20,16},{24,28},{28,24},{1,5},{5... | collective-permute-start | bytes 503816 | tf_op jit(solution)/shard_map/ppermute | solution.py:353
  37.9 7.2 %collective-permute-start.9 = (bf16[2,328,128]{2,1,0:T(8,128)(2,1)S(1)}, bf16[2,328,128]{2,1,0:T(8,128)(2,1)S(1)}, u32[]{:S(2)}, u32[]{:S(2)}) collective-permute-start(bf16[2,328,128]{2,1,0:T(8,128)(2,1)S(1)} %get-tuple-element.24), channel_id=1, source_target_pairs={{0,8},{4,12},{8,0},{12,4},{16,24},{20,28},{24,16},{28,20},{1,9},{5... | collective-permute-start | bytes 503816 | tf_op jit(solution)/shard_map/ppermute | solution.py:353
  38.3 9.8 %collective-permute-start.10 = (bf16[2,328,128]{2,1,0:T(8,128)(2,1)S(1)}, bf16[2,328,128]{2,1,0:T(8,128)(2,1)S(1)}, u32[]{:S(2)}, u32[]{:S(2)}) collective-permute-start(bf16[2,328,128]{2,1,0:T(8,128)(2,1)S(1)} %get-tuple-element.25), channel_id=1, source_target_pairs={{0,12},{4,8},{8,4},{12,0},{16,28},{20,24},{24,20},{28,16},{1,13},{... | collective-permute-start | bytes 503816 | tf_op jit(solution)/shard_map/ppermute | solution.py:353
  40.5 25.7 %collective-permute-start.7 = (bf16[192,896]{1,0:T(8,128)(2,1)S(1)}, bf16[192,896]{1,0:T(8,128)(2,1)S(1)}, u32[]{:S(2)}, u32[]{:S(2)}) collective-permute-start(bf16[192,896]{1,0:T(8,128)(2,1)S(1)} %collective-permute-done.6.x_ref), channel_id=1, source_target_pairs={{0,1},{1,0},{2,3},{3,2},{4,5},{5,4},{6,7},{7,6},{8,9},{9,8},{10,11... | collective-permute-start | bytes 1032200 | tf_op jit(solution)/shard_map/ppermute | solution.py:348
  48.2 6.3 %collective-permute-start.11 = (bf16[328,128]{1,0:T(8,128)(2,1)S(1)}, bf16[328,128]{1,0:T(8,128)(2,1)S(1)}, u32[]{:S(2)}, u32[]{:S(2)}) collective-permute-start(bf16[328,128]{1,0:T(8,128)(2,1)S(1)} %get-tuple-element.27), channel_id=1, source_target_pairs={{0,16},{4,20},{8,24},{12,28},{16,0},{20,4},{24,8},{28,12},{1,17},{... | collective-permute-start | bytes 251912 | tf_op jit(solution)/shard_map/ppermute | solution.py:353
  54.5 3.5 %collective-permute-start.14 = (f32[88,128]{1,0:T(8,128)S(1)}, f32[88,128]{1,0:T(8,128)S(1)}, u32[]{:S(2)}, u32[]{:S(2)}) collective-permute-start(f32[88,128]{1,0:T(8,128)S(1)} %shard_map.112.own_ref), channel_id=1, source_target_pairs={{0,3},{1,2},{2,1},{3,0},{4,7},{5,6},{6,5},{7,4},{8,11},{9,10},{10,... | collective-permute-start | bytes 135176 | tf_op jit(solution)/shard_map/ppermute | solution.py:348
  54.5 4.4 %collective-permute-start.13 = (f32[88,128]{1,0:T(8,128)S(1)}, f32[88,128]{1,0:T(8,128)S(1)}, u32[]{:S(2)}, u32[]{:S(2)}) collective-permute-start(f32[88,128]{1,0:T(8,128)S(1)} %shard_map.112.own_ref), channel_id=1, source_target_pairs={{0,2},{1,3},{2,0},{3,1},{4,6},{5,7},{6,4},{7,5},{8,10},{9,11},{10,... | collective-permute-start | bytes 135176 | tf_op jit(solution)/shard_map/ppermute | solution.py:348
  54.6 4.4 %collective-permute-start.12 = (f32[88,128]{1,0:T(8,128)S(1)}, f32[88,128]{1,0:T(8,128)S(1)}, u32[]{:S(2)}, u32[]{:S(2)}) collective-permute-start(f32[88,128]{1,0:T(8,128)S(1)} %shard_map.112.own_ref), channel_id=1, source_target_pairs={{0,1},{1,0},{2,3},{3,2},{4,5},{5,4},{6,7},{7,6},{8,9},{9,8},{10,11... | collective-permute-start | bytes 135176 | tf_op jit(solution)/shard_map/ppermute | solution.py:348
  59.7 6.5 %copy-start.1 = (bf16[192,2496]{1,0:T(8,128)(2,1)S(1)}, bf16[192,2496]{1,0:T(8,128)(2,1)}, u32[]{:S(2)}) copy-start(bf16[192,2496]{1,0:T(8,128)(2,1)} %gate_in.1) | copy-start | bytes 2875396

commit v2 on v1

--- a/solution.py
+++ b/solution.py
@@ -45,7 +45,7 @@
 
 
 def far_off():
-    return pl.BlockSpec(memory_space=pltpu.HBM)
+    return pl.BlockSpec(memory_space=pl.ANY)
 
 
 def call(kernel, outs, smem=(), hbm=(), args=(), flops=0, scratch=(), room=48000, hbm_outs=0):
@@ -86,48 +86,58 @@
         copy.wait()
 
 
-def act_kernel(groups, me_ref, gate_ref, up_ref, first_ref, second_ref, padded_ref, low_ref, mine_ref, hidden):
-    rows, width = gate_ref.shape
+def act_kernel(groups, chunk, gate_ref, up_ref, first_ref, second_ref, padded_ref, low_ref, mine_ref, gate, up, first, hidden, sems):
+    rows, width = gate.shape
     per = width // groups
     step = 16
-    mine_ref[...] = second_ref[:, columns(me_ref, 0, mine_ref.shape[1])]
-
-    def one(index, carry):
-        at = pl.ds(pl.multiple_of(index * step, step), step)
-        gate_vals = gate_ref[at, :].astype(F32)
-        silu = gate_vals * jax.nn.sigmoid(gate_vals)
-        hidden[at, :] = (silu * up_ref[at, :].astype(F32)).astype(BF16)
-        return carry
-
-    lax.fori_loop(0, rows // step, one, 0)
+    pieces = [pl.ds(at, chunk) for at in range(0, rows, chunk)]
+    coming = [
+        fetch([(gate_ref.at[at, :], gate.at[at, :]), (up_ref.at[at, :], up.at[at, :])], sems.at[n])
+        for n, at in enumerate(pieces)
+    ]
+    late = fetch([(first_ref, first), (second_ref.at[:, columns(0, mine_ref.shape[1])], mine_ref)], sems.at[len(pieces)])
     room = padded_ref.shape[2]
+    for n, piece in enumerate(pieces):
+        for copy in coming[n]:
+            copy.wait()
+
+        def one(index, carry, base=n * chunk):
+            at = pl.ds(pl.multiple_of(base + index * step, step), step)
+            gate_vals = gate[at, :].astype(F32)
+            silu = gate_vals * jax.nn.sigmoid(gate_vals)
+            hidden[at, :] = (silu * up[at, :].astype(F32)).astype(BF16)
+            return carry
+
+        lax.fori_loop(0, chunk // step, one, 0)
+    for copy in late:
+        copy.wait()
+    low_ref[...] = dot(hidden[...], first[...], NT)
     for group in range(groups):
         padded_ref[group, :, pl.ds(0, per)] = hidden[:, group * per : (group + 1) * per]
         if room > per:
             padded_ref[group, :, pl.ds(per, room - per)] = jnp.zeros((rows, room - per), BF16)
-    low_ref[...] = dot(hidden[...], first_ref[...], NT)
 
 
 def shaped(shape, dtype):
     return jax.ShapeDtypeStruct(shape, dtype)
 
 
-def columns(me, bit, width):
-    return pl.ds(pl.multiple_of((me[0] ^ bit) * width, LANES), width)
+def columns(bit, width):
+    return pl.ds(pl.multiple_of((lax.axis_index("mp") ^ bit) * width, LANES), width)
 
 
 def through_kernel(own_ref, second_ref, out_ref):
-    out_ref[...] = dot(own_ref[...], second_ref[...], NT).astype(BF16)
+    out_ref[...] = dot(own_ref[...], second_ref[...], NT)
 
 
 def add_kernel(one_ref, other_ref, out_ref):
-    out_ref[...] = one_ref[...] + other_ref[...]
+    out_ref[...] = (one_ref[...] + other_ref[...]).astype(out_ref.dtype)
 
 
 def make_share(groups, brows, width, rank, per):
     _, _, _, _, q, r, blocks, share, _ = layout_of(rank, per, brows, width)
 
-    def kernel(here_ref, x_ref, low_a, low_b, out_ref, prod):
+    def kernel(x_ref, low_a, low_b, out_ref, prod):
         low = (low_a[...] + low_b[...]).astype(BF16)
         prod[...] = dot(low, x_ref[...], TN)
         for group in range(groups):
@@ -156,13 +166,12 @@
 def make_send(groups, brows, width, rank, per):
     full_, rem, half, a_rows, _, _, _, _, b_rows = layout_of(rank, per, brows, width)
 
-    def kernel(here_ref, part_0, part_1, part_2, part_3, padded_ref, share_ref, through_ref, *outs):
-        parts = [part[...].astype(F32) for part in (part_0, part_1, part_2, part_3)]
-        through = ((parts[0] + parts[1]) + (parts[2] + parts[3])).astype(BF16)
+    def kernel(pair_0, pair_1, padded_ref, share_ref, through_ref, *outs):
+        through = (pair_0[...].astype(F32) + pair_1[...].astype(F32)).astype(BF16)
         through_ref[...] = through
         for peer, out_ref in enumerate(outs):
             for side in range(2):
-                group = here_ref[0] ^ (peer + side * len(outs))
+                group = lax.axis_index("dp") ^ (peer + side * len(outs))
                 piece = dot(through, padded_ref[group], TN)
                 for j in range(full_):
                     out_ref[side, pl.ds(j * rank, rank), :] = piece[:, j * LANES : (j + 1) * LANES].astype(BF16)
@@ -176,34 +185,35 @@
     return kernel
 
 
-def half_kernel(*refs):
-    *parts, mine_ref, other_ref = refs
-    for side in range(2):
-        total = parts[0][side].astype(F32)
-        for part in parts[1:]:
-            total = total + part[side].astype(F32)
-        if side:
-            other_ref[...] = total.astype(BF16)
-        else:
-            mine_ref[...] = total
-
-
-def make_sum_b(groups, brows, width, rank, per):
-    _, _, _, a_rows, _, _, _, _, b_rows = layout_of(rank, per, brows, width)
-
-    def kernel(mine_ref, other_ref, out_ref):
-        at = pl.ds(a_rows, b_rows)
-        out_ref[...] = mine_ref[at] + other_ref[at].astype(F32)
+def make_half(groups, brows, width, rank, per):
+    _, _, _, a_rows, _, _, _, _, _ = layout_of(rank, per, brows, width)
+
+    def kernel(*refs):
+        *parts, mine_ref, other_ref, b_ref = refs
+        for side in range(2):
+            total = parts[0][side].astype(F32)
+            for part in parts[1:]:
+                total = total + part[side].astype(F32)
+            b_ref[side] = total[a_rows:].astype(BF16)
+            if side:
+                other_ref[...] = total[:a_rows].astype(BF16)
+            else:
+                mine_ref[...] = total[:a_rows]
 
     return kernel
 
 
-def make_sum_a(groups, brows, width, rank, per):
-    full_, rem, half, a_rows, *_ = layout_of(rank, per, brows, width)
-
-    def kernel(mine_ref, other_ref, a_ref, total):
-        at = pl.ds(0, a_rows)
-        total[...] = mine_ref[at] + other_ref[at].astype(F32)
+def gather_kernel(*refs):
+    *parts, out_ref = refs
+    for at, part in enumerate(parts):
+        out_ref[at] = part[1]
+
+
+def make_finish(groups, brows, width, rank, per):
+    full_, rem, half, _, q, r, blocks, share, _ = layout_of(rank, per, brows, width)
+
+    def kernel(mine_ref, other_ref, own_ref, core_ref, x_ref, far_ref, landed_ref, a_ref, b_ref, total, part):
+        total[...] = mine_ref[...] + other_ref[...].astype(F32)
         for j in range(full_):
             a_ref[0, :, pl.ds(j * LANES, LANES)] = total[pl.ds(j * rank, rank), :]
         if rem:
@@ -214,39 +224,32 @@
                 a_ref[0, pl.ds(rank // 2, rank // 2), at] = pltpu.roll(last, LANES // 2, 1)[:, :rem]
             else:
                 a_ref[0, :, at] = total[pl.ds(full_ * rank, rank), :][:, :rem]
-
-    return kernel
-
-
-def make_join(groups, brows, width, rank, per):
-    _, _, _, _, q, r, blocks, share, _ = layout_of(rank, per, brows, width)
-
-    def kernel(me_ref, own_ref, core_ref, x_ref, far_ref, out_ref):
         for bit, ref in enumerate((own_ref, core_ref, x_ref, far_ref)):
-            base = (me_ref[0] ^ bit) * width
+            part[...] = ref[0].astype(F32) + landed_ref[bit].astype(F32)
+            base = (lax.axis_index("mp") ^ bit) * width
             at = 0
             for j in range(blocks):
                 cols = pl.ds(pl.multiple_of(base + j * LANES, LANES), LANES)
                 for k in range(q):
-                    out_ref[pl.ds(k * SUB, SUB), cols] = ref[pl.ds(at, SUB), :]
+                    b_ref[pl.ds(k * SUB, SUB), cols] = part[pl.ds(at, SUB), :]
                     at += SUB
             if r:
                 for j in range(0, blocks, share):
                     for i in range(j, min(j + share, blocks)):
                         cols = pl.ds(pl.multiple_of(base + i * LANES, LANES), LANES)
-                        out_ref[pl.ds(q * SUB, r), cols] = ref[pl.ds(at + (i - j) * r, r), :]
+                        b_ref[pl.ds(q * SUB, r), cols] = part[pl.ds(at + (i - j) * r, r), :]
                     at += SUB
 
     return kernel
 
 
 def near_kernel(
-    tile, me_ref, first_ref, weight_ref, own_ref, core_ref, through_ref, out_ref, first, weight, total, arrive, leave
+    tile, first_ref, weight_ref, own_ref, core_ref, through_ref, out_ref, first, weight, total, arrive, leave
 ):
     hid = weight_ref.shape[0]
     width = own_ref.shape[1]
     spans = [pl.ds(at, min(tile, hid - at)) for at in range(0, hid, tile)]
-    coming = fetch([(weight_ref.at[:, columns(me_ref, bit, width)], weight.at[bit]) for bit in range(2)], arrive)
+    coming = fetch([(weight_ref.at[:, columns(bit, width)], weight.at[bit]) for bit in range(2)], arrive)
     small = fetch([(first_ref, first)], arrive.at[pl.ds(2, 1)])
     small[0].wait()
     for span in spans:
@@ -263,7 +266,7 @@
 
 
 def distant_kernel(
-    tile, me_ref, weight_ref, total_ref, gate_in, up_in, x_ref, far_ref, gate_ref, up_ref,
+    tile, weight_ref, total_ref, gate_in, up_in, x_ref, far_ref, gate_ref, up_ref,
     weight, total, gate, up, grad_gate, grad_up, arrive, leave,
 ):
     hid = weight_ref.shape[0]
@@ -271,9 +274,9 @@
     spans = [pl.ds(at, min(tile, hid - at)) for at in range(0, hid, tile)]
     coming = fetch(
         [
-            (weight_ref.at[:, columns(me_ref, 2, width)], weight.at[0]),
+            (weight_ref.at[:, columns(2, width)], weight.at[0]),
             (total_ref, total),
-            (weight_ref.at[:, columns(me_ref, 3, width)], weight.at[1]),
+            (weight_ref.at[:, columns(3, width)], weight.at[1]),
             (gate_in, gate),
             (up_in, up),
         ],
@@ -298,16 +301,15 @@
         copy.wait()
 
 
-def near_call(me, own, core, through, first_t, weight, tile=512):
+def near_call(own, core, through, first_t, weight, tile=512):
     rows, width = own.shape
     hid = weight.shape[0]
     rank = through.shape[1]
     return call(
         functools.partial(near_kernel, tile),
         [shaped((rows, hid), F32)],
-        [me],
-        [first_t, weight],
-        [own, core, through],
+        hbm=[first_t, weight],
+        args=[own, core, through],
         flops=4 * rows * hid * width,
         scratch=[
             pltpu.VMEM((rank, hid), BF16),
@@ -321,15 +323,14 @@
     )
 
 
-def distant_call(me, total, other, far, weight, gate, up, tile=512):
+def distant_call(total, other, far, weight, gate, up, tile=512):
     rows, width = other.shape
     hid = weight.shape[0]
     return call(
         functools.partial(distant_kernel, tile),
         [shaped((rows, hid), BF16)] * 2,
-        [me],
-        [weight, total, gate, up],
-        [other, far],
+        hbm=[weight, total, gate, up],
+        args=[other, far],
         flops=4 * rows * hid * width,
         scratch=[
             pltpu.VMEM((2, hid, width), BF16),
@@ -365,8 +366,6 @@
     hid, rank = adapter_first.shape
     per, brows = hid // groups, rank // groups
     tall = tokens // owned
-    me = lax.axis_index("mp").astype(jnp.int32).reshape(1)
-    here = lax.axis_index("dp").astype(jnp.int32).reshape(1)
     first_t = adapter_first.T
     room = -(-per // LANES) * LANES
     _, _, _, a_rows, _, _, _, _, b_rows = layout_of(rank, per, brows, width)
@@ -387,32 +386,36 @@
     )
     packed = lax.all_to_all(outgoing, "dp", split_axis=0, concat_axis=0, tiled=True).reshape(tokens, width)
 
+    chunk = tokens // 4 if tokens % 64 == 0 else tokens
     padded, low_0, second = call(
-        functools.partial(act_kernel, groups),
+        functools.partial(act_kernel, groups, chunk),
         [
             shaped((groups, tokens, room), BF16),
             shaped((tokens, rank), F32),
             shaped((rank, width), BF16),
         ],
-        [me],
-        args=[gate_preactivation, up_preactivation, first_t, adapter_second],
+        hbm=[gate_preactivation, up_preactivation, first_t, adapter_second],
         flops=2 * tokens * hid * rank,
-        scratch=[pltpu.VMEM((tokens, hid), BF16)],
+        scratch=[
+            pltpu.VMEM((tokens, hid), BF16),
+            pltpu.VMEM((tokens, hid), BF16),
+            pltpu.VMEM((rank, hid), BF16),
+            pltpu.VMEM((tokens, hid), BF16),
+            pltpu.SemaphoreType.DMA((tokens // chunk + 1, 2)),
+        ],
+        room=11000,
     )
     low_1 = swap(low_0, 1)
     low_a = call(add_kernel, [shaped((tokens, rank), F32)], args=[low_0, low_1])
     low_b = swap(low_a, 2)
 
-    part_0 = call(
-        through_kernel, [shaped((tokens, rank), BF16)], args=[packed, second], flops=2 * tokens * width * rank
-    )
-    part_2 = swap(part_0, 2)
-    part_3 = swap(part_0, 3)
+    part_0 = call(through_kernel, [shaped((tokens, rank), F32)], args=[packed, second], flops=2 * tokens * width * rank)
     part_1 = swap(part_0, 1)
+    pair_0 = call(add_kernel, [shaped((tokens, rank), BF16)], args=[part_0, part_1])
+    pair_1 = swap(pair_0, 2)
     share = call(
         make_share(*sizes),
         [shaped((groups, b_rows, LANES), BF16)],
-        [here],
         args=[packed, low_a, low_b],
         scratch=[pltpu.VMEM((rank, width), F32)],
     )
@@ -423,33 +426,33 @@
     through, *payload = call(
         make_send(*sizes),
         [shaped((tokens, rank), BF16)] + [shaped((2, a_rows + b_rows, LANES), BF16)] * peers,
-        [here],
-        args=[part_0, part_1, part_2, part_3, padded, share],
+        args=[pair_0, pair_1, padded, share],
         flops=2 * tokens * hid * rank,
     )
     arrived = [payload[0]]
     for peer in range(1, peers):
         arrived.append(trade(payload[peer], peer))
 
-    total = near_call(me, packed, core, through, first_t, down_weight)
-    far = swap(side, 1)
-    mine, other = call(
-        half_kernel, [shaped((a_rows + b_rows, LANES), F32), shaped((a_rows + b_rows, LANES), BF16)], args=arrived
-    )
-    landed = trade(other, peers)
-    grad_gate, grad_up = distant_call(me, total, side, far, down_weight, gate_preactivation, up_preactivation)
-
-    b_0 = call(make_sum_b(*sizes), [shaped((b_rows, LANES), F32)], args=[mine, landed])
+    total = near_call(packed, core, through, first_t, down_weight)
+    mine, other, b_0 = call(
+        make_half(*sizes),
+        [shaped((a_rows, LANES), F32), shaped((a_rows, LANES), BF16), shaped((2, b_rows, LANES), BF16)],
+        args=arrived,
+    )
     b_3 = swap(b_0, 3)
     b_2 = swap(b_0, 2)
     b_1 = swap(b_0, 1)
-    grad_a_t = call(
-        make_sum_a(*sizes),
-        [shaped((1, rank, per), F32)],
-        args=[mine, landed],
-        scratch=[pltpu.VMEM((a_rows, LANES), F32)],
-    )
-    grad_b = call(make_join(*sizes), [shaped((brows, 4 * width), F32)], [me], args=[b_0, b_1, b_2, b_3])
+    landed = trade(other, peers)
+    far = swap(side, 1)
+    b_all = call(gather_kernel, [shaped((4, b_rows, LANES), BF16)], args=[b_0, b_1, b_2, b_3])
+    b_landed = trade(b_all, peers)
+    grad_gate, grad_up = distant_call(total, side, far, down_weight, gate_preactivation, up_preactivation)
+    grad_a_t, grad_b = call(
+        make_finish(*sizes),
+        [shaped((1, rank, per), F32), shaped((brows, 4 * width), F32)],
+        args=[mine, landed, b_0, b_1, b_2, b_3, b_landed],
+        scratch=[pltpu.VMEM((a_rows, LANES), F32), pltpu.VMEM((b_rows, LANES), F32)],
+    )
     return grad_gate, grad_up, jnp.swapaxes(grad_a_t, 1, 2), grad_b
 
 

time: 73.8 us -> 66.6 us (0.902)
  waiting for transfers between devices: 19.9 us -> 12.8 us
  local copies, waits for them, and re-layouts: 4.54 us -> 1.04 us
  starting transfers between devices: 10.6 us -> 12.4 us
  Pallas kernels: 19.1 us -> 20.8 us
    ppermute x4 -> x5, waiting for transfers between devices: 13.1 us -> 6.88 us  [trade(): return lax.ppermute(value, 'dp', [(i, i ^ bit) for i in range(count)])]
    unnamed x12 -> x6, local copies, waits for them, and re-layouts: 4.54 us -> 1.04 us
    ppermute x4 -> x5, starting transfers between devices: 4.39 us -> 6.35 us  [trade(): return lax.ppermute(value, 'dp', [(i, i ^ bit) for i in range(count)])]
    pallas_call x12, Pallas kernels: 19.1 us -> 20.8 us  [call(): pl.pallas_call(kernel, out_shape=list(outs), in_specs=[sspec() for _ in s...]
    ppermute x11 -> x10, waiting for transfers between devices: 6.81 us -> 5.95 us  [swap(): return lax.ppermute(value, 'mp', [(i, i ^ bit) for i in range(count)])]
    ppermute x11 -> x10, starting transfers between devices: 6.23 us -> 6.05 us  [swap(): return lax.ppermute(value, 'mp', [(i, i ^ bit) for i in range(count)])]
  transfers between devices with their start and end apart: 15 -> 15, of which waited for: 9 -> 10; matrix products, arithmetic and copies ran while one was open for 0% -> 0% of each run, Pallas kernels for 14% -> 18%
where the time goes in v2:
time: 66.6 us; the launch traced here: 66.3 us
  Pallas kernels  20.8 us (31%)
  blocking collectives  18.5 us (28%)
  waiting for transfers between devices  12.8 us (19%)
  starting transfers between devices  12.4 us (19%)
  local copies, waits for them, and re-layouts  1.04 us (2%)
  between operations  0.73 us (1%)
    pallas_call x12, Pallas kernels, call(): pl.pallas_call(kernel, out_shape=list(outs), in_specs=[sspec() for _ in s...  20.8 us
    all_to_all x1, blocking collectives, fast_layer(): lax.all_to_all(outgoing, 'dp', split_axis=0, concat_axis=0, tiled=True)  18.5 us
    ppermute x5, waiting for transfers between devices, trade(): return lax.ppermute(value, 'dp', [(i, i ^ bit) for i in range(count)])  6.88 us
    ppermute x5, starting transfers between devices, trade(): return lax.ppermute(value, 'dp', [(i, i ^ bit) for i in range(count)])  6.35 us
    ppermute x10, starting transfers between devices, swap(): return lax.ppermute(value, 'mp', [(i, i ^ bit) for i in range(count)])  6.05 us
    ppermute x10, waiting for transfers between devices, swap(): return lax.ppermute(value, 'mp', [(i, i ^ bit) for i in range(count)])  5.95 us
  transfers between devices with their start and end apart: 15, of which 10 were waited for; matrix products, arithmetic and copies ran while one was open for 0% of the time, Pallas kernels for 18%

profile of v2, /device:TPU:0, one launch (start us, length us, event | category | flops | bytes accessed | tf_op | source)
XLA Modules:
  0.0 66.3 jit_solution(7774469704433229393)
XLA Ops:
  0.6 1.9 %shard_map.102 = bf16[24,8,896]{2,1,0:T(8,128)(2,1)} custom-call(s32[24]{0:T(128)} %plan_ref.1, bf16[24,8,896]{2,1,0:T(8,128)(2,1)} %bitcast.11), custom_call_target="tpu_custom_call" | custom-call | bytes 688224 | tf_op jit(solution)/shard_map/pallas_call | solution.py:53
  2.5 18.5 %all_to_all.5 = bf16[24,8,896]{2,1,0:T(8,128)(2,1)S(1)} all-to-all(bf16[24,8,896]{2,1,0:T(8,128)(2,1)} %shard_map.102), channel_id=1, replica_groups=mesh['dp'=8,'mp'=4] {'dp'}, dimensions={0} | all-to-all | bytes 688128 | tf_op jit(solution)/shard_map/all_to_all | solution.py:387
  21.1 1.5 %collective-permute-start.5 = (bf16[192,896]{1,0:T(8,128)(2,1)S(1)}, bf16[192,896]{1,0:T(8,128)(2,1)S(1)}, u32[]{:S(2)}, u32[]{:S(2)}) collective-permute-start(bf16[192,896]{1,0:T(8,128)(2,1)S(1)} %bitcast.4), channel_id=1, source_target_pairs={{0,2},{1,3},{2,0},{3,1},{4,6},{5,7},{6,4},{7,5},{8,10},{9,11},{10,... | collective-permute-start | bytes 1032200 | tf_op jit(solution)/shard_map/ppermute | solution.py:349
  22.5 0.0 copy-start.1
  22.6 1.0 %copy-done.1 = bf16[2496,96]{0,1:T(8,128)(2,1)S(1)} copy-done((bf16[2496,96]{0,1:T(8,128)(2,1)S(1)}, bf16[2496,96]{0,1:T(8,128)(2,1)}, u32[]{:S(2)}) %copy-start.1) | copy-done | bytes 479256
  23.6 3.3 %shard_map.103 = (bf16[8,192,384]{2,1,0:T(8,128)(2,1)}, f32[192,96]{1,0:T(8,128)S(1)}, bf16[96,896]{1,0:T(8,128)(2,1)S(1)}) custom-call(bf16[192,2496]{1,0:T(8,128)(2,1)} %gate_in.1, bf16[192,2496]{1,0:T(8,128)(2,1)} %up_in.1, bf16[96,2496]{1,0:T(8,128)(2,1)S(1)} %bitcast.9, bf16[96,3584]{1,0:T(8,128)(2,1)} %second_ref.1), custom_call_target="tpu_custom_call" | custom-call | flops 92012544 | bytes 4509696 | tf_op jit(solution)/shard_map/pallas_call | solution.py:53
  26.9 0.0 copy-start.2
  26.9 0.1 collective-permute-start.3
  27.0 0.5 collective-permute-start
  27.5 0.3 shard_map.104.one_ref
  27.7 0.1 collective-permute-start.1
  27.9 0.4 collective-permute-done.3.other_ref
  28.3 0.6 collective-permute-start.4
  28.9 0.2 collective-permute-done.1.other_ref
  29.1 1.3 %collective-permute-start.2 = (bf16[192,96]{1,0:T(8,128)(2,1)S(1)}, bf16[192,96]{1,0:T(8,128)(2,1)S(1)}, u32[]{:S(2)}, u32[]{:S(2)}) collective-permute-start(bf16[192,96]{1,0:T(8,128)(2,1)S(1)} %shard_map.105.pair_0), channel_id=1, source_target_pairs={{0,2},{1,3},{2,0},{3,1},{4,6},{5,7},{6,4},{7,5},{8,10},{9,11},{10,... | collective-permute-start | bytes 110600 | tf_op jit(solution)/shard_map/ppermute | solution.py:349
  30.5 3.3 %collective-permute-done.4.low_b = f32[192,96]{1,0:T(8,128)S(1)} collective-permute-done((f32[192,96]{1,0:T(8,128)S(1)}, f32[192,96]{1,0:T(8,128)S(1)}, u32[]{:S(2)}, u32[]{:S(2)}) %collective-permute-start.4) | collective-permute-done | bytes 73760 | tf_op jit(solution)/shard_map/ppermute | solution.py:349
  33.7 0.2 shard_map.107.share_ref
  34.0 0.3 collective-permute-done.2.pair_1
  34.3 0.0 copy-done.2
  34.3 0.5 shard_map.108
  34.7 0.9 %collective-permute-start.7 = (bf16[2,328,128]{2,1,0:T(8,128)(2,1)S(1)}, bf16[2,328,128]{2,1,0:T(8,128)(2,1)S(1)}, u32[]{:S(2)}, u32[]{:S(2)}) collective-permute-start(bf16[2,328,128]{2,1,0:T(8,128)(2,1)S(1)} %get-tuple-element.26), channel_id=1, source_target_pairs={{0,4},{4,0},{8,12},{12,8},{16,20},{20,16},{24,28},{28,24},{1,5},{5... | collective-permute-start | bytes 503816 | tf_op jit(solution)/shard_map/ppermute | solution.py:354
  35.7 0.3 collective-permute-start.8
  36.0 2.2 %collective-permute-start.9 = (bf16[2,328,128]{2,1,0:T(8,128)(2,1)S(1)}, bf16[2,328,128]{2,1,0:T(8,128)(2,1)S(1)}, u32[]{:S(2)}, u32[]{:S(2)}) collective-permute-start(bf16[2,328,128]{2,1,0:T(8,128)(2,1)S(1)} %get-tuple-element.28), channel_id=1, source_target_pairs={{0,12},{4,8},{8,4},{12,0},{16,28},{20,24},{24,20},{28,16},{1,13},{... | collective-permute-start | bytes 503816 | tf_op jit(solution)/shard_map/ppermute | solution.py:354
  38.3 0.0 collective-permute-done.5.x_ref
  38.3 0.0 collective-permute-start.6
  38.3 2.8 %collective-permute-done.7.refs_1_ = bf16[2,328,128]{2,1,0:T(8,128)(2,1)S(1)} collective-permute-done((bf16[2,328,128]{2,1,0:T(8,128)(2,1)S(1)}, bf16[2,328,128]{2,1,0:T(8,128)(2,1)S(1)}, u32[]{:S(2)}, u32[]{:S(2)}) %collective-permute-start.7) | collective-permute-done | bytes 167968 | tf_op jit(solution)/shard_map/ppermute | solution.py:354
  41.0 1.6 %collective-permute-done.8.refs_2_ = bf16[2,328,128]{2,1,0:T(8,128)(2,1)S(1)} collective-permute-done((bf16[2,328,128]{2,1,0:T(8,128)(2,1)S(1)}, bf16[2,328,128]{2,1,0:T(8,128)(2,1)S(1)}, u32[]{:S(2)}, u32[]{:S(2)}) %collective-permute-start.8) | collective-permute-done | bytes 167968 | tf_op jit(solution)/shard_map/ppermute | solution.py:354
  42.7 2.4 %collective-permute-done.9.refs_3_ = bf16[2,328,128]{2,1,0:T(8,128)(2,1)S(1)} collective-permute-done((bf16[2,328,128]{2,1,0:T(8,128)(2,1)S(1)}, bf16[2,328,128]{2,1,0:T(8,128)(2,1)S(1)}, u32[]{:S(2)}, u32[]{:S(2)}) %collective-permute-start.9) | collective-permute-done | bytes 167968 | tf_op jit(solution)/shard_map/ppermute | solution.py:354
  45.1 0.1 shard_map.111
  45.2 0.1 collective-permute-start.13
  45.2 0.6 collective-permute-start.12
  45.8 1.2 %collective-permute-start.11 = (bf16[2,88,128]{2,1,0:T(8,128)(2,1)S(1)}, bf16[2,88,128]{2,1,0:T(8,128)(2,1)S(1)}, u32[]{:S(2)}, u32[]{:S(2)}) collective-permute-start(bf16[2,88,128]{2,1,0:T(8,128)(2,1)S(1)} %get-tuple-element.31.refs_0_.own_ref), channel_id=1, source_target_pairs={{0,1},{1,0},{2,3},{3,2},{4,5},{5,4},{6,7},{7,6},{8,9},{9,8},{10,11... | collective-permute-start | bytes 135176 | tf_op jit(solution)/shard_map/ppermute | solution.py:349
  47.1 1.6 %collective-permute-done.13.refs_3_.far_ref = bf16[2,88,128]{2,1,0:T(8,128)(2,1)S(1)} collective-permute-done((bf16[2,88,128]{2,1,0:T(8,128)(2,1)S(1)}, bf16[2,88,128]{2,1,0:T(8,128)(2,1)S(1)}, u32[]{:S(2)}, u32[]{:S(2)}) %collective-permute-start.13) | collective-permute-done | bytes 45088 | tf_op jit(solution)/shard_map/ppermute | solution.py:349
  48.7 0.8 %collective-permute-start.10 = (bf16[240,128]{1,0:T(8,128)(2,1)S(1)}, bf16[240,128]{1,0:T(8,128)(2,1)S(1)}, u32[]{:S(2)}, u32[]{:S(2)}) collective-permute-start(bf16[240,128]{1,0:T(8,128)(2,1)S(1)} %get-tuple-element.30), channel_id=1, source_target_pairs={{0,16},{4,20},{8,24},{12,28},{16,0},{20,4},{24,8},{28,12},{1,17},{... | collective-permute-start | bytes 184328 | tf_op jit(solution)/shard_map/ppermute | solution.py:354
  49.5 0.2 collective-permute-done.12.refs_2_.x_ref
  49.7 0.0 collective-permute-done.11.refs_1_.core_ref
  49.7 2.0 %collective-permute-start.14 = (bf16[4,88,128]{2,1,0:T(8,128)(2,1)S(1)}, bf16[4,88,128]{2,1,0:T(8,128)(2,1)S(1)}, u32[]{:S(2)}, u32[]{:S(2)}) collective-permute-start(bf16[4,88,128]{2,1,0:T(8,128)(2,1)S(1)} %shard_map.112), channel_id=1, source_target_pairs={{0,16},{4,20},{8,24},{12,28},{16,0},{20,4},{24,8},{28,12},{1,17},{... | collective-permute-start | bytes 270344 | tf_op jit(solution)/shard_map/ppermute | solution.py:354
  51.7 0.0 collective-permute-done.core_ref
  51.7 0.0 copy-start
  51.7 6.5 %shard_map.109.total_ref = f32[192,2496]{1,0:T(8,128)} custom-call(bf16[96,2496]{1,0:T(8,128)(2,1)S(1)} %bitcast.10, bf16[2496,3584]{1,0:T(8,128)(2,1)} %weight_ref.3, bf16[192,896]{1,0:T(8,128)(2,1)S(1)} %bitcast.8, bf16[192,896]{1,0:T(8,128)(2,1)S(1)} %collective-permute-done.core_ref, bf16[192,96]{1,0:T(8,128)(2,1)S(1)} %get-tuple-element.22.through_ref), custom_call_target="tpu_custom_call" | custom-call | flops 1717567488 | bytes 21012480 | tf_op jit(solution)/shard_map/pallas_call | solution.py:53
  58.2 0.0 collective-permute-done.10.other_ref
  58.2 0.1 collective-permute-done.14.landed_ref
  58.3 0.8 %shard_map.113 = (f32[1,96,312]{2,1,0:T(8,128)}, f32[12,3584]{1,0:T(8,128)}) custom-call(f32[240,128]{1,0:T(8,128)S(1)} %get-tuple-element.29.mine_ref, bf16[240,128]{1,0:T(8,128)(2,1)S(1)} %collective-permute-done.10.other_ref, bf16[2,88,128]{2,1,0:T(8,128)(2,1)S(1)} %get-tuple-element.31.refs_0_.own_ref, ...), custom_call_target="tpu_custom_call" | custom-call | bytes 746496 | tf_op jit(solution)/shard_map/pallas_call | solution.py:53
  59.1 0.0 collective-permute-done.6.far_ref
  59.1 0.0 copy-done
  59.1 7.1 %shard_map.110 = (bf16[192,2496]{1,0:T(8,128)(2,1)}, bf16[192,2496]{1,0:T(8,128)(2,1)}) custom-call(bf16[2496,3584]{1,0:T(8,128)(2,1)} %weight_ref.3, f32[192,2496]{1,0:T(8,128)} %shard_map.109.total_ref, bf16[192,2496]{1,0:T(8,128)(2,1)S(1)} %copy-done, bf16[192,2496]{1,0:T(8,128)(2,1)} %up_in.1, bf16[192,896]{1,0:T(8,128)(2,1)S(1)} %collective-permute-done.5.x_ref, ...), custom_call_target="tpu_custom_call" | custom-call | flops 1717567488 | bytes 24330240 | tf_op jit(solution)/shard_map/pallas_call | solution.py:53
  (3 shorter events, 0.0 us)
Async XLA Ops:
  21.1 17.2 %collective-permute-start.5 = (bf16[192,896]{1,0:T(8,128)(2,1)S(1)}, bf16[192,896]{1,0:T(8,128)(2,1)S(1)}, u32[]{:S(2)}, u32[]{:S(2)}) collective-permute-start(bf16[192,896]{1,0:T(8,128)(2,1)S(1)} %bitcast.4), channel_id=1, source_target_pairs={{0,2},{1,3},{2,0},{3,1},{4,6},{5,7},{6,4},{7,5},{8,10},{9,11},{10,... | collective-permute-start | bytes 1032200 | tf_op jit(solution)/shard_map/ppermute | solution.py:349
  22.5 1.0 %copy-start.1 = (bf16[2496,96]{0,1:T(8,128)(2,1)S(1)}, bf16[2496,96]{0,1:T(8,128)(2,1)}, u32[]{:S(2)}) copy-start(bf16[2496,96]{0,1:T(8,128)(2,1)} %param.11) | copy-start | bytes 1437700
  26.9 7.4 %copy-start.2 = (bf16[8,192,384]{2,1,0:T(8,128)(2,1)S(1)}, bf16[8,192,384]{2,1,0:T(8,128)(2,1)}, u32[]{:S(2)}) copy-start(bf16[8,192,384]{2,1,0:T(8,128)(2,1)} %get-tuple-element.20.padded_ref) | copy-start | bytes 3538948
  26.9 1.4 %collective-permute-start.3 = (f32[192,96]{1,0:T(8,128)S(1)}, f32[192,96]{1,0:T(8,128)S(1)}, u32[]{:S(2)}, u32[]{:S(2)}) collective-permute-start(f32[192,96]{1,0:T(8,128)S(1)} %get-tuple-element.21.one_ref), channel_id=1, source_target_pairs={{0,1},{1,0},{2,3},{3,2},{4,5},{5,4},{6,7},{7,6},{8,9},{9,8},{10,11... | collective-permute-start | bytes 221192 | tf_op jit(solution)/shard_map/ppermute | solution.py:349
  27.0 24.7 %collective-permute-start = (bf16[192,896]{1,0:T(8,128)(2,1)S(1)}, bf16[192,896]{1,0:T(8,128)(2,1)S(1)}, u32[]{:S(2)}, u32[]{:S(2)}) collective-permute-start(bf16[192,896]{1,0:T(8,128)(2,1)S(1)} %bitcast.5), channel_id=1, source_target_pairs={{0,1},{1,0},{2,3},{3,2},{4,5},{5,4},{6,7},{7,6},{8,9},{9,8},{10,11... | collective-permute-start | bytes 1032200 | tf_op jit(solution)/shard_map/ppermute | solution.py:349
  27.7 1.4 %collective-permute-start.1 = (f32[192,96]{1,0:T(8,128)S(1)}, f32[192,96]{1,0:T(8,128)S(1)}, u32[]{:S(2)}, u32[]{:S(2)}) collective-permute-start(f32[192,96]{1,0:T(8,128)S(1)} %shard_map.104.one_ref), channel_id=1, source_target_pairs={{0,1},{1,0},{2,3},{3,2},{4,5},{5,4},{6,7},{7,6},{8,9},{9,8},{10,11... | collective-permute-start | bytes 221192 | tf_op jit(solution)/shard_map/ppermute | solution.py:349
  28.3 5.4 %collective-permute-start.4 = (f32[192,96]{1,0:T(8,128)S(1)}, f32[192,96]{1,0:T(8,128)S(1)}, u32[]{:S(2)}, u32[]{:S(2)}) collective-permute-start(f32[192,96]{1,0:T(8,128)S(1)} %shard_map.106.low_a), channel_id=1, source_target_pairs={{0,2},{1,3},{2,0},{3,1},{4,6},{5,7},{6,4},{7,5},{8,10},{9,11},{10,... | collective-permute-start | bytes 221192 | tf_op jit(solution)/shard_map/ppermute | solution.py:349
  29.1 5.1 %collective-permute-start.2 = (bf16[192,96]{1,0:T(8,128)(2,1)S(1)}, bf16[192,96]{1,0:T(8,128)(2,1)S(1)}, u32[]{:S(2)}, u32[]{:S(2)}) collective-permute-start(bf16[192,96]{1,0:T(8,128)(2,1)S(1)} %shard_map.105.pair_0), channel_id=1, source_target_pairs={{0,2},{1,3},{2,0},{3,1},{4,6},{5,7},{6,4},{7,5},{8,10},{9,11},{10,... | collective-permute-start | bytes 110600 | tf_op jit(solution)/shard_map/ppermute | solution.py:349
  34.7 6.3 %collective-permute-start.7 = (bf16[2,328,128]{2,1,0:T(8,128)(2,1)S(1)}, bf16[2,328,128]{2,1,0:T(8,128)(2,1)S(1)}, u32[]{:S(2)}, u32[]{:S(2)}) collective-permute-start(bf16[2,328,128]{2,1,0:T(8,128)(2,1)S(1)} %get-tuple-element.26), channel_id=1, source_target_pairs={{0,4},{4,0},{8,12},{12,8},{16,20},{20,16},{24,28},{28,24},{1,5},{5... | collective-permute-start | bytes 503816 | tf_op jit(solution)/shard_map/ppermute | solution.py:354
  35.7 7.0 %collective-permute-start.8 = (bf16[2,328,128]{2,1,0:T(8,128)(2,1)S(1)}, bf16[2,328,128]{2,1,0:T(8,128)(2,1)S(1)}, u32[]{:S(2)}, u32[]{:S(2)}) collective-permute-start(bf16[2,328,128]{2,1,0:T(8,128)(2,1)S(1)} %get-tuple-element.27), channel_id=1, source_target_pairs={{0,8},{4,12},{8,0},{12,4},{16,24},{20,28},{24,16},{28,20},{1,9},{5... | collective-permute-start | bytes 503816 | tf_op jit(solution)/shard_map/ppermute | solution.py:354
  36.0 9.0 %collective-permute-start.9 = (bf16[2,328,128]{2,1,0:T(8,128)(2,1)S(1)}, bf16[2,328,128]{2,1,0:T(8,128)(2,1)S(1)}, u32[]{:S(2)}, u32[]{:S(2)}) collective-permute-start(bf16[2,328,128]{2,1,0:T(8,128)(2,1)S(1)} %get-tuple-element.28), channel_id=1, source_target_pairs={{0,12},{4,8},{8,4},{12,0},{16,28},{20,24},{24,20},{28,16},{1,13},{... | collective-permute-start | bytes 503816 | tf_op jit(solution)/shard_map/ppermute | solution.py:354
  38.3 20.8 %collective-permute-start.6 = (bf16[192,896]{1,0:T(8,128)(2,1)S(1)}, bf16[192,896]{1,0:T(8,128)(2,1)S(1)}, u32[]{:S(2)}, u32[]{:S(2)}) collective-permute-start(bf16[192,896]{1,0:T(8,128)(2,1)S(1)} %collective-permute-done.5.x_ref), channel_id=1, source_target_pairs={{0,1},{1,0},{2,3},{3,2},{4,5},{5,4},{6,7},{7,6},{8,9},{9,8},{10,11... | collective-permute-start | bytes 1032200 | tf_op jit(solution)/shard_map/ppermute | solution.py:349
  45.2 3.5 %collective-permute-start.13 = (bf16[2,88,128]{2,1,0:T(8,128)(2,1)S(1)}, bf16[2,88,128]{2,1,0:T(8,128)(2,1)S(1)}, u32[]{:S(2)}, u32[]{:S(2)}) collective-permute-start(bf16[2,88,128]{2,1,0:T(8,128)(2,1)S(1)} %get-tuple-element.31.refs_0_.own_ref), channel_id=1, source_target_pairs={{0,3},{1,2},{2,1},{3,0},{4,7},{5,6},{6,5},{7,4},{8,11},{9,10},{10,... | collective-permute-start | bytes 135176 | tf_op jit(solution)/shard_map/ppermute | solution.py:349
  45.2 4.4 %collective-permute-start.12 = (bf16[2,88,128]{2,1,0:T(8,128)(2,1)S(1)}, bf16[2,88,128]{2,1,0:T(8,128)(2,1)S(1)}, u32[]{:S(2)}, u32[]{:S(2)}) collective-permute-start(bf16[2,88,128]{2,1,0:T(8,128)(2,1)S(1)} %get-tuple-element.31.refs_0_.own_ref), channel_id=1, source_target_pairs={{0,2},{1,3},{2,0},{3,1},{4,6},{5,7},{6,4},{7,5},{8,10},{9,11},{10,... | collective-permute-start | bytes 135176 | tf_op jit(solution)/shard_map/ppermute | solution.py:349
  45.8 3.8 %collective-permute-start.11 = (bf16[2,88,128]{2,1,0:T(8,128)(2,1)S(1)}, bf16[2,88,128]{2,1,0:T(8,128)(2,1)S(1)}, u32[]{:S(2)}, u32[]{:S(2)}) collective-permute-start(bf16[2,88,128]{2,1,0:T(8,128)(2,1)S(1)} %get-tuple-element.31.refs_0_.own_ref), channel_id=1, source_target_pairs={{0,1},{1,0},{2,3},{3,2},{4,5},{5,4},{6,7},{7,6},{8,9},{9,8},{10,11... | collective-permute-start | bytes 135176 | tf_op jit(solution)/shard_map/ppermute | solution.py:349
  48.7 9.5 %collective-permute-start.10 = (bf16[240,128]{1,0:T(8,128)(2,1)S(1)}, bf16[240,128]{1,0:T(8,128)(2,1)S(1)}, u32[]{:S(2)}, u32[]{:S(2)}) collective-permute-start(bf16[240,128]{1,0:T(8,128)(2,1)S(1)} %get-tuple-element.30), channel_id=1, source_target_pairs={{0,16},{4,20},{8,24},{12,28},{16,0},{20,4},{24,8},{28,12},{1,17},{... | collective-permute-start | bytes 184328 | tf_op jit(solution)/shard_map/ppermute | solution.py:354
  49.7 8.7 %collective-permute-start.14 = (bf16[4,88,128]{2,1,0:T(8,128)(2,1)S(1)}, bf16[4,88,128]{2,1,0:T(8,128)(2,1)S(1)}, u32[]{:S(2)}, u32[]{:S(2)}) collective-permute-start(bf16[4,88,128]{2,1,0:T(8,128)(2,1)S(1)} %shard_map.112), channel_id=1, source_target_pairs={{0,16},{4,20},{8,24},{12,28},{16,0},{20,4},{24,8},{28,12},{1,17},{... | collective-permute-start | bytes 270344 | tf_op jit(solution)/shard_map/ppermute | solution.py:354
  51.7 7.4 %copy-start = (bf16[192,2496]{1,0:T(8,128)(2,1)S(1)}, bf16[192,2496]{1,0:T(8,128)(2,1)}, u32[]{:S(2)}) copy-start(bf16[192,2496]{1,0:T(8,128)(2,1)} %gate_in.1) | copy-start | bytes 2875396
